TPU v7x, 128 devices: a whole 4x4x4 slice. The times are simulated.
128 devices in a mesh: section: 2 (over z_lo), ex: 16 (over x, y), tp: 4 (over z_hi, core).
Axes of the slice: x: 4, y: 4, z: 4 (z_hi: 2, z_lo: 2; z = z_hi * 2 + z_lo), core: 2. Of those that a mesh axis runs over, the one named last changes fastest.
Arguments:
- activations: bfloat16 [2, 8192, 28672], P('section', 'ex', 'tp')
- out_grads: bfloat16 [2, 8192, 8192], P('section', 'ex', 'tp')
- lengths: int32 [64], P('ex'), may hold values from 16 to 128, as said below
Outputs:
- block_kernel: float32 [64, 4], P('ex')
- cross_kernel: float32 [64, 4], P('ex')
Inputs may be any that keep to these rules, and one draw needn't show every extreme that they name: `lengths`: some example has all 128 tokens live and some has 16.
All inputs are finite; a program needn't handle non-finite values.
Results may differ from a plain program's by a relative error of at most 0.0003.
Values may be sent and summed in bfloat16 or wider, within the bound.
A program may use at most 64 MiB of HBM per device.

v0:
```python
import jax
import jax.numpy as jnp
from jax import lax
from jax.sharding import PartitionSpec as P

D = 8192
FF = 28672
LEN = 128
EX_DEV = 4


def from_behind(value, axis, steps):
    count = lax.axis_size(axis)
    pairs = [(source, (source + steps) % count) for source in range(count)]
    return lax.ppermute(value, axis, pairs)


def cut_along(shard, dim, peers):
    lengths = shard.shape
    blocks = shard.reshape(*lengths[:dim], peers, lengths[dim] // peers, *lengths[dim + 1 :])
    return jnp.moveaxis(blocks, dim, 0)


def sent_and_summed(shard, axis, dim):
    peers = lax.axis_size(axis)
    blocks = lax.all_to_all(cut_along(shard, dim, peers), axis, 0, 0, tiled=True)
    return jnp.sum(blocks, axis=0)


def sent_together(arrays, axis, dim, along):
    ends, at = ([], 0)
    for a in arrays[:-1]:
        at += a.shape[along]
        ends.append(at)
    both = jnp.concatenate(arrays, axis=along)
    return tuple(jnp.split(sent_and_summed(both, axis, dim), ends, axis=along))


def sent_to_all(shard, axis):
    peers = lax.axis_size(axis)
    return lax.all_to_all(
        jnp.broadcast_to(shard[None], (peers, *shard.shape)), axis, 0, 0, tiled=True
    )


def taken_together(shard, axis):
    everything = sent_to_all(shard, axis)
    return jnp.sum(everything, axis=0)


def in_one(arrays, axis):
    ends = [0]
    for a in arrays:
        ends.append(ends[-1] + a.size)
    running = taken_together(jnp.concatenate([a.ravel() for a in arrays]), axis)
    return tuple((running[b:e].reshape(a.shape) for a, b, e in zip(arrays, ends, ends[1:])))


def gram_of(left, right):
    return lax.dot_general(
        left, right, (((1,), (1,)), ((), ())), preferred_element_type=jnp.float32
    )


def reduce_tile(left, product, right):
    inner = jnp.dot(product, right, precision=lax.Precision.HIGHEST)
    return jnp.dot(left.T, inner, precision=lax.Precision.HIGHEST)


def weights_from(counts, rows):
    slots = jnp.arange(LEN, dtype=jnp.int32)
    live = slots[None, :] < counts[:, None]
    inverse = 1.0 / jnp.sqrt(counts.astype(jnp.float32))
    weight = jnp.where(live, inverse[:, None], jnp.float32(0.0)).reshape(rows)
    member = (
        (jnp.arange(rows, dtype=jnp.int32) // LEN)[:, None]
        == jnp.arange(EX_DEV, dtype=jnp.int32)[None, :]
    ).astype(jnp.float32)
    return member * weight[:, None]


def on_device(activations, out_grads, lengths):
    feats = activations[0]
    grads = out_grads[0]
    rows = feats.shape[0]
    weighted = weights_from(lengths, rows)
    sent_lengths = lengths.astype(jnp.bfloat16)
    scale_x = 1.0 / jnp.sqrt(jnp.float32(FF))
    scale_g = 1.0 / jnp.sqrt(jnp.float32(D))
    diag_x = gram_of(feats, feats) * scale_x
    diag_g = gram_of(grads, grads) * scale_g
    half_axis = lax.axis_size("ex") // 2
    lower = lax.axis_index("ex") < half_axis
    half_x = feats.shape[1] // 2
    half_g = grads.shape[1] // 2
    keep_x = lax.dynamic_slice_in_dim(
        feats, jnp.where(lower, 0, half_x).astype(jnp.int32), half_x, 1
    )
    send_x = lax.dynamic_slice_in_dim(
        feats, jnp.where(lower, half_x, 0).astype(jnp.int32), half_x, 1
    )
    keep_g = lax.dynamic_slice_in_dim(
        grads, jnp.where(lower, 0, half_g).astype(jnp.int32), half_g, 1
    )
    send_g = lax.dynamic_slice_in_dim(
        grads, jnp.where(lower, half_g, 0).astype(jnp.int32), half_g, 1
    )
    far_x, far_g, far_len = from_behind((send_x, send_g, sent_lengths), "ex", half_axis)
    part_x = gram_of(keep_x, far_x)
    part_g = gram_of(keep_g, far_g)
    back_x, back_g = from_behind((part_x, part_g), "ex", half_axis)
    cross_x = (part_x + back_x.T) * scale_x
    cross_g = (part_g + back_g.T) * scale_g
    far_weighted = weights_from(far_len.astype(jnp.int32), rows)
    offdiag = 1.0 - jnp.eye(EX_DEV, dtype=jnp.float32)
    sum_dx, sum_dg, sum_cx, sum_cg = sent_together((diag_x, diag_g, cross_x, cross_g), "tp", 0, 1)
    share = rows // lax.axis_size("tp")
    start = lax.axis_index("tp") * share
    row_weights = lax.dynamic_slice_in_dim(weighted, start, share, 0)
    block = reduce_tile(row_weights, sum_dx * sum_dg, weighted) * offdiag
    cross = reduce_tile(row_weights, sum_cx * sum_cg, far_weighted)
    block, cross = in_one((block, cross), ("section", "tp"))
    return (block, cross)


def solution(mesh):
    placed = (P("section", "ex", "tp"), P("section", "ex", "tp"), P("ex"))
    return jax.shard_map(
        on_device,
        mesh=mesh,
        in_specs=placed,
        out_specs=(P("ex", None), P("ex", None)),
        check_vma=False,
    )
```

profile of v0, /device:TPU:1, one launch (start us, length us, event | category | flops | bytes accessed | tf_op | source)
XLA Modules:
  0.0 234.3 jit_solution(12774290628765769898)
XLA Ops:
  0.7 4.3 %dynamic-slice_bitcast_fusion = bf16[512,3584]{1,0:T(8,128)(2,1)} fusion(bf16[1,512,7168]{2,1,0:T(8,128)(2,1)} %param.3, s32[]{:T(128)S(6)} %select_n.58), kind=kLoop, calls=%fused_computation.6 | loop fusion | bytes 7340036 | tf_op jit(solution)/shard_map/dynamic_slice | solution.py:99
  4.9 3.6 %collective-permute-start = (bf16[512,3584]{1,0:T(8,128)(2,1)}, bf16[512,3584]{1,0:T(8,128)(2,1)}, u32[]{:S(2)}, u32[]{:S(2)}) collective-permute-start(bf16[512,3584]{1,0:T(8,128)(2,1)} %dynamic-slice_bitcast_fusion), channel_id=1, source_target_pairs={{0,32},{4,36},{8,40},{12,44},{16,48},{20,52},{24,56},{28,60},{32,0... | collective-permute-start | bytes 11010056 | tf_op jit(solution)/shard_map/ppermute | solution.py:15
  8.5 0.1 dynamic-slice_bitcast_fusion.1
  8.6 0.1 collective-permute-start.2
  8.7 2.3 fusion.10
  11.0 98.9 %collective-permute-done.2 = bf16[512,1024]{1,0:T(8,128)(2,1)} collective-permute-done((bf16[512,1024]{1,0:T(8,128)(2,1)S(1)}, bf16[512,1024]{1,0:T(8,128)(2,1)}, u32[]{:S(2)}, u32[]{:S(2)}) %collective-permute-start.2) | collective-permute-done | bytes 1048608 | tf_op jit(solution)/shard_map/ppermute | solution.py:15
  109.9 2.0 fusion.14
  111.8 1.4 copy.16
  113.2 3.1 %collective-permute-start.3 = (f32[512,512]{1,0:T(8,128)}, f32[512,512]{1,0:T(8,128)}, u32[]{:S(2)}, u32[]{:S(2)}) collective-permute-start(f32[512,512]{1,0:T(8,128)} %copy.16), channel_id=1, source_target_pairs={{0,32},{4,36},{8,40},{12,44},{16,48},{20,52},{24,56},{28,60},{32,0... | collective-permute-start | bytes 3145736 | tf_op jit(solution)/shard_map/ppermute | solution.py:15
  116.3 6.2 %fusion.2 = f32[512,512]{0,1:T(8,128)} fusion(bf16[512,3584]{1,0:T(8,128)(2,1)} %collective-permute-done, bf16[1,512,7168]{2,1,0:T(8,128)(2,1)} %param.3, s32[]{:T(128)S(6)} %select_n.57), kind=kOutput, calls=%fused_computation.4 | convolution fusion | flops 1879048192 | bytes 8388612 | tf_op jit(solution)/shard_map/dot_general | solution.py:60
  122.6 2.6 %copy.15 = f32[512,512]{1,0:T(8,128)} copy(f32[512,512]{0,1:T(8,128)} %fusion.2) | data formatting | bytes 2097152 | tf_op jit(solution)/shard_map/dot_general | solution.py:60
  125.2 9.4 %fusion.7 = f32[512,512]{0,1:T(8,128)S(1)} fusion(bf16[1,512,7168]{2,1,0:T(8,128)(2,1)} %param.3), kind=kOutput, calls=%fused_computation.10 | convolution fusion | flops 3758358528 | bytes 8388608 | tf_op jit(solution)/shard_map/dot_general | solution.py:60
  134.6 3.7 %collective-permute-done.3 = f32[512,512]{1,0:T(8,128)} collective-permute-done((f32[512,512]{1,0:T(8,128)}, f32[512,512]{1,0:T(8,128)}, u32[]{:S(2)}, u32[]{:S(2)}) %collective-permute-start.3) | collective-permute-done | bytes 1048608 | tf_op jit(solution)/shard_map/ppermute | solution.py:15
  138.3 1.4 fusion.13
  139.8 20.9 %collective-permute-done.1 = f32[512,512]{1,0:T(8,128)S(1)} collective-permute-done((f32[512,512]{1,0:T(8,128)}, f32[512,512]{1,0:T(8,128)S(1)}, u32[]{:S(2)}, u32[]{:S(2)}) %collective-permute-start.1) | collective-permute-done | bytes 1048608 | tf_op jit(solution)/shard_map/ppermute | solution.py:15
  160.7 0.2 fusion.16
  160.9 2.2 copy_bitcast_fusion
  163.2 8.0 %all-to-all-start = ((f32[4,128,2048]{1,2,0:T(8,128)}), f32[4,128,2048]{1,2,0:T(8,128)}, u32[]{:S(2)}, u32[]{:S(2)}) async-start(f32[4,128,2048]{1,2,0:T(8,128)} %copy_bitcast_fusion), calls=%async_computation | async-start | bytes 8388608 | tf_op jit(solution)/shard_map/all_to_all | solution.py:26
  171.1 2.8 %collective-permute-start.4 = (bf16[4]{0:T(256)(128)(2,1)S(1)}, bf16[4]{0:T(256)(128)(2,1)S(1)}, u32[]{:S(2)}, u32[]{:S(2)}) collective-permute-start(bf16[4]{0:T(256)(128)(2,1)S(1)} %convert_element_type.19), channel_id=1, source_target_pairs={{0,32},{4,36},{8,40},{12,44},{16,48},{20,52},{24,56},{28,60},{32,0... | collective-permute-start | bytes 32 | tf_op jit(solution)/shard_map/ppermute | solution.py:15
  174.0 0.2 fusion.23
  174.2 0.9 collective-permute-done.4
  175.1 44.8 %all-to-all-done = f32[4,128,2048]{1,2,0:T(8,128)} async-done(((f32[4,128,2048]{1,2,0:T(8,128)}), f32[4,128,2048]{1,2,0:T(8,128)}, u32[]{:S(2)}, u32[]{:S(2)}) %all-to-all-start) | async-done | bytes 4194336 | tf_op jit(solution)/shard_map/all_to_all | solution.py:26
  220.0 2.5 %reduce_sum.18 = f32[128,2048]{0,1:T(8,128)S(1)} reduce(f32[4,128,2048]{1,2,0:T(8,128)} %all-to-all-done, f32[]{:T(128)} %constant.48.clone.1), dimensions={0}, to_apply=%region_0.1 | reduce | flops 786432 | bytes 5242884 | tf_op jit(solution)/shard_map/reduce_sum | solution.py:27
  222.5 0.7 fusion.20
  223.2 0.7 fusion.18
  223.9 0.2 fusion.28
  224.1 0.1 reshape.110
  224.2 0.3 convolution_multiply_fusion
  224.6 0.1 pad_maximum_fusion
  224.7 8.1 %all_to_all.11 = f32[8,1,32]{2,1,0:T(1,128)S(1)} all-to-all(f32[8,1,32]{2,1,0:T(1,128)S(1)} %broadcast_in_dim.37), channel_id=1, replica_groups=mesh['section'=2,'ex'=16,'tp'=4] {'section','tp'}, dimensions={0} | all-to-all | bytes 2048 | tf_op jit(solution)/shard_map/all_to_all | solution.py:41
  232.9 0.7 reshape.111
  233.6 0.7 reshape.112
  (21 shorter events, 0.4 us)
Async XLA Ops:
  0.6 7.9 %copy-start = (bf16[1,512,2048]{2,1,0:T(8,128)(2,1)S(1)}, bf16[1,512,2048]{2,1,0:T(8,128)(2,1)}, u32[]{:S(2)}) copy-start(bf16[1,512,2048]{2,1,0:T(8,128)(2,1)} %param.4) | copy-start | bytes 6291460
  4.9 111.4 %collective-permute-start = (bf16[512,3584]{1,0:T(8,128)(2,1)}, bf16[512,3584]{1,0:T(8,128)(2,1)}, u32[]{:S(2)}, u32[]{:S(2)}) collective-permute-start(bf16[512,3584]{1,0:T(8,128)(2,1)} %dynamic-slice_bitcast_fusion), channel_id=1, source_target_pairs={{0,32},{4,36},{8,40},{12,44},{16,48},{20,52},{24,56},{28,60},{32,0... | collective-permute-start | bytes 11010056 | tf_op jit(solution)/shard_map/ppermute | solution.py:15
  8.6 101.3 %collective-permute-start.2 = (bf16[512,1024]{1,0:T(8,128)(2,1)S(1)}, bf16[512,1024]{1,0:T(8,128)(2,1)}, u32[]{:S(2)}, u32[]{:S(2)}) collective-permute-start(bf16[512,1024]{1,0:T(8,128)(2,1)S(1)} %dynamic-slice_bitcast_fusion.1), channel_id=1, source_target_pairs={{0,32},{4,36},{8,40},{12,44},{16,48},{20,52},{24,56},{28,60},{32,0... | collective-permute-start | bytes 3145736 | tf_op jit(solution)/shard_map/ppermute | solution.py:15
  113.2 25.1 %collective-permute-start.3 = (f32[512,512]{1,0:T(8,128)}, f32[512,512]{1,0:T(8,128)}, u32[]{:S(2)}, u32[]{:S(2)}) collective-permute-start(f32[512,512]{1,0:T(8,128)} %copy.16), channel_id=1, source_target_pairs={{0,32},{4,36},{8,40},{12,44},{16,48},{20,52},{24,56},{28,60},{32,0... | collective-permute-start | bytes 3145736 | tf_op jit(solution)/shard_map/ppermute | solution.py:15
  125.2 35.5 %copy-start.1 = (f32[512,512]{0,1:T(8,128)S(1)}, f32[512,512]{0,1:T(8,128)}, u32[]{:S(2)}) copy-start(f32[512,512]{0,1:T(8,128)} %fusion.2) | copy-start | bytes 3145732
  125.2 35.5 %collective-permute-start.1 = (f32[512,512]{1,0:T(8,128)}, f32[512,512]{1,0:T(8,128)S(1)}, u32[]{:S(2)}, u32[]{:S(2)}) collective-permute-start(f32[512,512]{1,0:T(8,128)} %copy.15), channel_id=1, source_target_pairs={{0,32},{4,36},{8,40},{12,44},{16,48},{20,52},{24,56},{28,60},{32,0... | collective-permute-start | bytes 3145736 | tf_op jit(solution)/shard_map/ppermute | solution.py:15
  134.6 26.3 %copy-start.2 = (f32[512,512]{0,1:T(8,128)S(1)}, f32[512,512]{0,1:T(8,128)}, u32[]{:S(2)}) copy-start(f32[512,512]{0,1:T(8,128)} %fusion.10) | copy-start | bytes 3145732
  163.2 8.0 %copy-start.3 = (s32[4]{0:T(128)S(1)}, s32[4]{0:T(128)}, u32[]{:S(2)}) copy-start(s32[4]{0:T(128)} %param.5) | copy-start | bytes 52
  163.2 56.8 %all-to-all-start = ((f32[4,128,2048]{1,2,0:T(8,128)}), f32[4,128,2048]{1,2,0:T(8,128)}, u32[]{:S(2)}, u32[]{:S(2)}) async-start(f32[4,128,2048]{1,2,0:T(8,128)} %copy_bitcast_fusion), calls=%async_computation | async-start | bytes 8388608 | tf_op jit(solution)/shard_map/all_to_all | solution.py:26
  171.1 3.9 %collective-permute-start.4 = (bf16[4]{0:T(256)(128)(2,1)S(1)}, bf16[4]{0:T(256)(128)(2,1)S(1)}, u32[]{:S(2)}, u32[]{:S(2)}) collective-permute-start(bf16[4]{0:T(256)(128)(2,1)S(1)} %convert_element_type.19), channel_id=1, source_target_pairs={{0,32},{4,36},{8,40},{12,44},{16,48},{20,52},{24,56},{28,60},{32,0... | collective-permute-start | bytes 32 | tf_op jit(solution)/shard_map/ppermute | solution.py:15
where the time goes:
time: 235 us; the launch traced here: 234 us
  waiting for transfers between devices  169 us (72%)
  matrix products  21.8 us (9%)
  starting transfers between devices  17.5 us (7%)
  local copies, waits for them, and re-layouts  9.91 us (4%)
  blocking collectives  8.14 us (3%)
  other arithmetic  6.96 us (3%)
    ppermute x5, waiting for transfers between devices, from_behind(): return lax.ppermute(value, axis, pairs)  124 us
    all_to_all x1, waiting for transfers between devices, sent_and_summed(): lax.all_to_all(cut_along(shard, dim, peers), axis, 0, 0, tiled=True)  44.8 us
    dot_general x4, matrix products, gram_of(): lax.dot_general(left, right, (((1,), (1,)), ((), ())), preferred_element_...  19.9 us
    ppermute x5, starting transfers between devices, from_behind(): return lax.ppermute(value, axis, pairs)  9.56 us
    all_to_all x1, blocking collectives, sent_to_all(): lax.all_to_all(jnp.broadcast_to(shard[None], (peers, *shard.shape)), axis...  8.14 us
    all_to_all x1, starting transfers between devices, sent_and_summed(): lax.all_to_all(cut_along(shard, dim, peers), axis, 0, 0, tiled=True)  7.97 us
  transfers between devices with their start and end apart: 6, of which 5 were waited for; matrix products, arithmetic and copies ran while one was open for 11% of the time, Pallas kernels for 0%

commit v1 on v0

v1 whole, which is shorter than its diff:
```python
import functools

import jax
import jax.numpy as jnp
from jax import lax
from jax.experimental import pallas as pl
from jax.experimental.pallas import tpu as pltpu
from jax.sharding import PartitionSpec as P

D = 8192
FF = 28672
LEN = 128
EX_DEV = 4
ROWS = EX_DEV * LEN
WIDE = 512
N_X = 7
N_G = 2
BASE = 128
STEP = 32
MESH = pl.DeviceIdType.MESH
F32 = jnp.float32
BF16 = jnp.bfloat16


def dot_nt(left, right):
    return lax.dot_general(left, right, (((1,), (1,)), ((), ())), preferred_element_type=F32)


def place():
    s = lax.axis_index("section")
    e = lax.axis_index("ex")
    t = lax.axis_index("tp")
    return s, e, t


def remote(src, dst, send, recv, device):
    return pltpu.make_async_remote_copy(
        src_ref=src, dst_ref=dst, send_sem=send, recv_sem=recv, device_id=device, device_id_type=MESH
    )


def greet(peers):
    barrier = pltpu.get_barrier_semaphore()
    for peer in peers:
        pl.semaphore_signal(barrier, inc=1, device_id=peer, device_id_type=MESH)
    return lambda: pl.semaphore_wait(barrier, len(peers))


def iota(shape, dim):
    return lax.broadcasted_iota(jnp.int32, shape, dim)


def block_tiles(rows_ref, j, out_ref):
    at = 0
    for a in range(EX_DEV - 1):
        width = (EX_DEV - 1 - a) * LEN
        out_ref[:, at : at + width] += dot_nt(
            rows_ref[j, a * LEN : (a + 1) * LEN, :], rows_ref[j, (a + 1) * LEN :, :]
        )
        at += width


def first_kernel(
    lens, x_hbm, g_hbm,
    ok_hbm, tl_hbm, gk_hbm, gs_hbm, p1_ref, blk_ref, far_len_ref, most_ref,
    xraw, graw, xs, xk, gs, gk, far, pick, xd, gd, r_core, r_z, r_back, lt, mt, lx, ly,
    ld_sem, out_sem, s_send, s_recv, d_send, d_recv, l_send, l_recv,
):
    s, e, t = place()
    x, y = e // 4, lax.rem(e, 4)
    hi = e // 8
    core, z = lax.rem(t, 2), t // 2
    partner = (s, lax.rem(e + 8, 16), t)
    core_peer = (s, e, t + 1 - 2 * core)
    z_peer = (s, e, lax.rem(t + 2, 4))
    x_peers = [(s, lax.rem(x + d, 4) * 4 + y, t) for d in (1, 2, 3)]
    y_peers = [(s, x * 4 + lax.rem(y + d, 4), t) for d in (1, 2, 3)]
    met = greet(x_peers + y_peers + [core_peer, z_peer])

    def load_x(j):
        half = jnp.where(j < N_X, 1 - hi, hi)
        at = pl.multiple_of((half * N_X + lax.rem(j, N_X)) * WIDE, WIDE)
        return pltpu.make_async_copy(x_hbm.at[:, pl.ds(at, WIDE)], xraw.at[j], ld_sem.at[j])

    def load_g(j):
        half = 1 - hi if j < N_G else hi
        at = pl.multiple_of((half * N_G + j % N_G) * WIDE, WIDE)
        return pltpu.make_async_copy(g_hbm.at[:, pl.ds(at, WIDE)], graw.at[j], ld_sem.at[2 * N_X + j])

    for j in range(N_X):
        load_x(j).start()
    for j in range(2 * N_G):
        load_g(j).start()
    for j in range(N_X, 2 * N_X):
        load_x(j).start()

    counts = [lens[j] for j in range(EX_DEV)]
    starts = [jnp.int32(0)]
    for j in range(EX_DEV):
        starts.append(starts[-1] + counts[j])
    row = iota((8, LEN), 0)
    mine = jnp.full((8, LEN), starts[EX_DEV], jnp.int32)
    for j in range(EX_DEV):
        mine = jnp.where(row == j, counts[j], mine)
    lt[...] = mine
    for b in range(EX_DEV):
        packed = iota((LEN, LEN), 0) + b * LEN
        source = jnp.full((LEN, LEN), -1, jnp.int32)
        for j in reversed(range(EX_DEV)):
            source = jnp.where(packed < starts[j + 1], packed - starts[j] + j * LEN, source)
        for c in range(EX_DEV):
            pick[b * LEN : (b + 1) * LEN, c * LEN : (c + 1) * LEN] = jnp.where(
                source == iota((LEN, LEN), 1) + c * LEN, 1.0, 0.0
            ).astype(BF16)

    met()
    for i, peer in enumerate(x_peers):
        remote(lt, lx.at[i], l_send.at[i], l_recv.at[i], peer).start()

    def send_x(c):
        return remote(xs.at[c, pl.ds(0, BASE), :], far.at[c], s_send.at[c], s_recv.at[c], partner)

    def pack_sent(c, carry):
        load_x(c).wait()
        xs[c] = jnp.dot(pick[...], xraw[c], preferred_element_type=F32).astype(BF16)

        @pl.when(c > 0)
        def _():
            send_x(c - 1).start()

        return carry

    lax.fori_loop(0, N_X, pack_sent, 0)

    xd[...] = jnp.zeros_like(xd)
    gd[...] = jnp.zeros_like(gd)
    for j in range(2 * N_G):
        load_g(j).wait()
    send_x(N_X - 1).start()

    def gram_g(j, carry):
        block_tiles(graw, j, gd)
        return carry

    lax.fori_loop(0, 2 * N_G, gram_g, 0)
    half = LEN // 2
    keep = pl.multiple_of(core * half, half)
    give = pl.multiple_of((1 - core) * half, half)
    to_core = remote(gd.at[pl.ds(give, half)], r_core, d_send.at[0], d_recv.at[0], core_peer)
    to_core.start()

    for i in range(3):
        remote(lt, lx.at[i], l_send.at[i], l_recv.at[i], x_peers[i]).wait_recv()
    mt[...] = jnp.maximum(jnp.maximum(lt[...], lx[0]), jnp.maximum(lx[1], lx[2]))
    far_len_ref[...] = lx[1]
    def pack_g(j, carry):
        gs[j] = jnp.dot(pick[...], graw[j], preferred_element_type=F32).astype(BF16)
        gk[j] = jnp.dot(pick[...], graw[N_G + j], preferred_element_type=F32).astype(BF16)
        return carry

    lax.fori_loop(0, N_G, pack_g, 0)
    for i, peer in enumerate(y_peers):
        remote(mt, ly.at[i], l_send.at[3 + i], l_recv.at[3 + i], peer).start()

    to_core.wait()
    gd[pl.ds(keep, half), :] += r_core[...]

    def pack_kept(c, carry):
        load_x(N_X + c).wait()
        xk[c] = jnp.dot(pick[...], xraw[N_X + c], preferred_element_type=F32).astype(BF16)
        return carry

    lax.fori_loop(0, N_X, pack_kept, 0)
    to_z = remote(gd.at[pl.ds(keep, half)], r_z, d_send.at[1], d_recv.at[1], z_peer)
    to_z.start()
    outs = [
        pltpu.make_async_copy(xk, ok_hbm, out_sem.at[0]),
        pltpu.make_async_copy(xs.at[:, pl.ds(BASE, ROWS - BASE), :], tl_hbm, out_sem.at[1]),
        pltpu.make_async_copy(gk, gk_hbm, out_sem.at[2]),
        pltpu.make_async_copy(gs, gs_hbm, out_sem.at[3]),
    ]
    for out in outs:
        out.start()

    def gram_x(j, carry):
        block_tiles(xraw, j, xd)
        return carry

    lax.fori_loop(0, 2 * N_X, gram_x, 0)
    for i in range(3):
        remote(mt, ly.at[i], l_send.at[3 + i], l_recv.at[3 + i], y_peers[i]).wait_recv()
    most_ref[...] = jnp.maximum(jnp.maximum(mt[...], ly[0]), jnp.maximum(ly[1], ly[2]))

    to_z.wait()
    gd[pl.ds(keep, half), :] += r_z[...]
    p1_ref[...] = jnp.zeros_like(p1_ref)
    back = remote(gd.at[pl.ds(keep, half)], r_back, d_send.at[2], d_recv.at[2], core_peer)

    def gram_far(c, carry):
        send_x(c).wait_recv()
        p1_ref[...] += dot_nt(far[c], xk[c])
        return carry

    gram_far(0, 0)
    back.start()
    back.wait()
    gd[pl.ds(give, half), :] = r_back[...]
    blk = jnp.zeros((8, LEN), F32)
    lane = iota((8, LEN), 1)
    inner_row = iota((LEN, LEN), 0)
    inner_lane = iota((LEN, LEN), 1)
    scale_x = 1.0 / jnp.sqrt(jnp.full((LEN, LEN), float(FF), F32))
    scale_g = 1.0 / jnp.sqrt(jnp.full((LEN, LEN), float(D), F32))
    inverse = [1.0 / jnp.sqrt(jnp.full((8, LEN), counts[j].astype(F32), F32)) for j in range(EX_DEV)]
    at = 0
    for a in range(EX_DEV - 1):
        for b in range(a + 1, EX_DEV):
            product = (xd[:, at : at + LEN] * scale_x) * (gd[:, at : at + LEN] * scale_g)
            live = (inner_row < counts[a]) & (inner_lane < counts[b])
            product = jnp.where(live, product, 0.0)
            total = jnp.sum(jnp.sum(product, axis=0, keepdims=True), axis=1, keepdims=True)
            spot = ((row == a) & (lane == 8 + b)) | ((row == b) & (lane == 8 + a))
            blk = blk + jnp.where(spot, jnp.broadcast_to(total, (8, LEN)) * inverse[a] * inverse[b], 0.0)
            at += LEN
    blk_ref[...] = blk
    lax.fori_loop(1, N_X, gram_far, 0)

    def sent(c, carry):
        send_x(c).wait_send()
        return carry

    lax.fori_loop(0, N_X, sent, 0)
    for i in range(3):
        remote(lt, lx.at[i], l_send.at[i], l_recv.at[i], x_peers[i]).wait_send()
        remote(mt, ly.at[i], l_send.at[3 + i], l_recv.at[3 + i], y_peers[i]).wait_send()
    for out in outs:
        out.wait()


def second_kernel(
    size, lens, far_len, blk_ref, p1_ref, gs_hbm, gk_hbm, ok_hbm, tl_hbm,
    block_ref, cross_ref,
    own, gb, cp, cf, gg, r1, r2, r3, farx, prod, wl, acc, tile, gather, total, last,
    ld_sem, g_send, g_recv, x_send, x_recv, r_send, r_recv, t_send, t_recv,
):
    s, e, t = place()
    hi = e // 8
    core, z = lax.rem(t, 2), t // 2
    partner = (s, lax.rem(e + 8, 16), t)
    core_peer = (s, e, t + 1 - 2 * core)
    z_peer = (s, e, lax.rem(t + 2, 4))
    me = s * 4 + t
    column = []
    for d in range(1, 8):
        other = lax.rem(me + d, 8)
        column.append((other // 4, e, lax.rem(other, 4)))
    met = greet([partner] + column)
    chunks = (size - BASE) // STEP
    loads = [
        pltpu.make_async_copy(gk_hbm, gb.at[1 - hi], ld_sem.at[0]),
        pltpu.make_async_copy(ok_hbm, own, ld_sem.at[1]),
    ]
    for load in loads:
        load.start()
    met()

    def send_g(c):
        return remote(
            gs_hbm.at[c, pl.ds(0, size), :], gb.at[1 - hi, c, pl.ds(0, size), :], g_send.at[c], g_recv.at[c], partner
        )

    def got_g(c):
        return remote(
            gs_hbm.at[c, pl.ds(0, size), :], gb.at[hi, c, pl.ds(0, size), :], g_send.at[c], g_recv.at[c], partner
        )

    def send_x(c):
        at = c * STEP if isinstance(c, int) else pl.multiple_of(c * STEP, STEP)
        return remote(tl_hbm.at[:, pl.ds(at, STEP), :], farx.at[c], x_send.at[c], x_recv.at[c], partner)

    for c in range(N_G):
        send_g(c).start()
    send_x(0).start()
    send_x(1).start()

    if size < ROWS:
        gb[hi, :, size:, :] = jnp.zeros((N_G, ROWS - size, WIDE), BF16)
        cf[size:, :] = jnp.zeros((ROWS - size, ROWS), F32)
    acc[...] = jnp.zeros_like(acc)
    begin = jnp.zeros((1, LEN), jnp.int32)
    for a in range(EX_DEV):
        count = far_len[a : a + 1, :]
        inverse = 1.0 / jnp.sqrt(count.astype(F32))
        rows = iota((size, LEN), 0)
        wl[a] = jnp.where((rows >= begin) & (rows < begin + count), inverse, 0.0)
        begin = begin + count
    for load in loads:
        load.wait()

    for c in range(N_G):
        got_g(c).wait_recv()
    half, quarter = size // 2, size // 4
    for c in range(N_G):
        part = dot_nt(gb[0, c, :size, :], gb[1, c])
        cp[...] = part if c == 0 else cp[...] + part
    keep_half = pl.multiple_of(core * half, 8)
    give_half = pl.multiple_of((1 - core) * half, 8)
    keep = pl.multiple_of(core * half + z * quarter, 8)
    give = pl.multiple_of(core * half + (1 - z) * quarter, 8)

    step = remote(cp.at[pl.ds(give_half, half)], r1, r_send.at[0], r_recv.at[0], core_peer)
    step.start()
    step.wait()
    cp[pl.ds(keep_half, half), :] += r1[...]
    to_z = remote(cp.at[pl.ds(give, quarter)], r2, r_send.at[1], r_recv.at[1], z_peer)
    to_z.start()

    def take(c):
        send_x(c).wait()
        if isinstance(c, int):
            if c + 2 < chunks:
                send_x(c + 2).start()
        else:
            @pl.when(c + 2 < chunks)
            def _():
                send_x(c + 2).start()

        def add(k, total):
            return total + dot_nt(farx[c, k], own[k])

        return lax.fori_loop(0, N_X, add, jnp.zeros((STEP, ROWS), F32))

    scale_x = 1.0 / jnp.sqrt(jnp.full((STEP, LEN), float(FF), F32))

    def weigh(part, at):
        for b in range(EX_DEV):
            lanes = slice(b * LEN, (b + 1) * LEN)
            product = (part[:, lanes] * scale_x) * gg[pl.ds(at, STEP), lanes]
            for a in range(EX_DEV):
                acc[a : a + 1, lanes] += jnp.sum(product * wl[a, pl.ds(at, STEP), :], axis=0, keepdims=True)

    prod[0:STEP, :] = take(0)
    to_z.wait()
    cp[pl.ds(keep, quarter), :] += r2[...]
    to_x = remote(cp.at[pl.ds(keep, quarter)], r3, r_send.at[2], r_recv.at[2], partner)
    to_x.start()
    prod[STEP : 2 * STEP, :] = take(1)
    prod[2 * STEP : 3 * STEP, :] = take(2)
    to_x.wait()
    cf[pl.ds(keep, quarter), :] = cp[pl.ds(keep, quarter), :] + r3[...]
    back = remote(cf.at[pl.ds(keep, quarter)], cf.at[pl.ds(keep, quarter)], r_send.at[3], r_recv.at[3], z_peer)
    back.start()
    prod[3 * STEP : 4 * STEP, :] = take(3)
    back.wait_send()
    remote(cf.at[pl.ds(keep, quarter)], cf.at[pl.ds(give, quarter)], r_send.at[3], r_recv.at[3], z_peer).wait_recv()
    back = remote(cf.at[pl.ds(keep_half, half)], cf.at[pl.ds(keep_half, half)], r_send.at[4], r_recv.at[4], core_peer)
    back.start()
    back.wait_send()
    remote(
        cf.at[pl.ds(keep_half, half)], cf.at[pl.ds(give_half, half)], r_send.at[4], r_recv.at[4], core_peer
    ).wait_recv()
    scale_g = 1.0 / jnp.sqrt(jnp.full((LEN, ROWS), float(D), F32))

    @pl.when(hi == 0)
    def _():
        for i in range(EX_DEV):
            gg[i * LEN : (i + 1) * LEN, :] = cf[i * LEN : (i + 1) * LEN, :] * scale_g

    @pl.when(hi == 1)
    def _():
        for i in range(EX_DEV):
            for j in range(EX_DEV):
                turned = jnp.transpose(cf[j * LEN : (j + 1) * LEN, i * LEN : (i + 1) * LEN])
                gg[i * LEN : (i + 1) * LEN, j * LEN : (j + 1) * LEN] = turned * scale_g[:, :LEN]

    def weigh_base(i, carry):
        at = pl.multiple_of(i * STEP, STEP)
        weigh(p1_ref[pl.ds(at, STEP), :], at)
        return carry

    lax.fori_loop(0, BASE // STEP, weigh_base, 0)

    def weigh_kept(i, carry):
        at = pl.multiple_of(i * STEP, STEP)
        weigh(prod[pl.ds(at, STEP), :], pl.multiple_of(BASE + i * STEP, STEP))
        return carry

    lax.fori_loop(0, 4, weigh_kept, 0)

    def rest(c, carry):
        weigh(take(c), pl.multiple_of(BASE + c * STEP, STEP))
        return carry

    lax.fori_loop(4, chunks, rest, 0)

    lane = iota((8, LEN), 1)
    wide_row, wide_lane = iota((8, ROWS), 0), iota((8, ROWS), 1)
    right = jnp.zeros((8, ROWS), F32)
    begin = jnp.int32(0)
    for b in range(EX_DEV):
        count = lens[b]
        inverse = 1.0 / jnp.sqrt(jnp.full((8, ROWS), count.astype(F32), F32))
        inside = (wide_row == b) & (wide_lane >= begin) & (wide_lane < begin + count)
        right = jnp.where(inside, inverse, right)
        begin = begin + count
    found = acc[...]
    out = blk_ref[...]
    for a in range(EX_DEV):
        summed = jnp.sum(right * found[a : a + 1, :], axis=1, keepdims=True)
        out = out + jnp.where(lane == a, summed, 0.0)
        summed = jnp.sum(found * right[a : a + 1, :], axis=1, keepdims=True)
        out = out + jnp.where(lane == 4 + a, summed, 0.0)
    tile[...] = out
    sends = [
        remote(tile, gather.at[me], t_send.at[i], t_recv.at[me], peer) for i, peer in enumerate(column)
    ]
    for send in sends:
        send.start()
    gather[me] = out
    for d in range(1, 8):
        other = lax.rem(me + d, 8)
        remote(tile, gather.at[other], t_send.at[d - 1], t_recv.at[other], column[d - 1]).wait_recv()
    whole = gather[0]
    for i in range(1, 8):
        whole = whole + gather[i]
    total[...] = whole
    final = remote(total, last, t_send.at[7], t_recv.at[8], partner)
    final.start()
    block_ref[...] = whole[:4, 8:12]
    final.wait()
    cross_ref[...] = whole[:4, 0:4] + last[:4, 4:8]
    for send in sends:
        send.wait_send()
    for c in range(N_G):
        send_g(c).wait_send()


def vmem():
    return pl.BlockSpec(memory_space=pltpu.VMEM)


def hbm():
    return pl.BlockSpec(memory_space=pl.ANY)


def smem():
    return pl.BlockSpec(memory_space=pltpu.SMEM)


def run_first(lengths, feats, grads):
    dma = pltpu.SemaphoreType.DMA
    return pl.pallas_call(
        first_kernel,
        name="block_part",
        out_shape=(
            jax.ShapeDtypeStruct((N_X, ROWS, WIDE), BF16),
            jax.ShapeDtypeStruct((N_X, ROWS - BASE, WIDE), BF16),
            jax.ShapeDtypeStruct((N_G, ROWS, WIDE), BF16),
            jax.ShapeDtypeStruct((N_G, ROWS, WIDE), BF16),
            jax.ShapeDtypeStruct((BASE, ROWS), F32),
            jax.ShapeDtypeStruct((8, LEN), F32),
            jax.ShapeDtypeStruct((8, LEN), jnp.int32),
            jax.ShapeDtypeStruct((8, LEN), jnp.int32),
        ),
        in_specs=[smem(), hbm(), hbm()],
        out_specs=(hbm(), hbm(), hbm(), hbm(), vmem(), vmem(), vmem(), vmem()),
        scratch_shapes=[
            pltpu.VMEM((2 * N_X, ROWS, WIDE), BF16),
            pltpu.VMEM((2 * N_G, ROWS, WIDE), BF16),
            pltpu.VMEM((N_X, ROWS, WIDE), BF16),
            pltpu.VMEM((N_X, ROWS, WIDE), BF16),
            pltpu.VMEM((N_G, ROWS, WIDE), BF16),
            pltpu.VMEM((N_G, ROWS, WIDE), BF16),
            pltpu.VMEM((N_X, BASE, WIDE), BF16),
            pltpu.VMEM((ROWS, ROWS), BF16),
            pltpu.VMEM((LEN, 6 * LEN), F32),
            pltpu.VMEM((LEN, 6 * LEN), F32),
            pltpu.VMEM((LEN // 2, 6 * LEN), F32),
            pltpu.VMEM((LEN // 2, 6 * LEN), F32),
            pltpu.VMEM((LEN // 2, 6 * LEN), F32),
            pltpu.VMEM((8, LEN), jnp.int32),
            pltpu.VMEM((8, LEN), jnp.int32),
            pltpu.VMEM((3, 8, LEN), jnp.int32),
            pltpu.VMEM((3, 8, LEN), jnp.int32),
            dma((2 * N_X + 2 * N_G,)),
            dma((4,)),
            dma((N_X,)),
            dma((N_X,)),
            dma((3,)),
            dma((3,)),
            dma((6,)),
            dma((6,)),
        ],
        compiler_params=pltpu.CompilerParams(collective_id=0, has_side_effects=True, vmem_limit_bytes=56 << 20),
    )(lengths, feats, grads)


def run_second(size, lengths, far_len, blk, p1, gs, gk, ok, tl):
    dma = pltpu.SemaphoreType.DMA
    chunks = (size - BASE) // STEP
    return pl.pallas_call(
        functools.partial(second_kernel, size),
        name="cross_part_%d" % size,
        out_shape=(jax.ShapeDtypeStruct((4, 4), F32), jax.ShapeDtypeStruct((4, 4), F32)),
        in_specs=[smem(), vmem(), vmem(), vmem(), hbm(), hbm(), hbm(), hbm()],
        out_specs=(vmem(), vmem()),
        scratch_shapes=[
            pltpu.VMEM((N_X, ROWS, WIDE), BF16),
            pltpu.VMEM((2, N_G, ROWS, WIDE), BF16),
            pltpu.VMEM((size, ROWS), F32),
            pltpu.VMEM((ROWS, ROWS), F32),
            pltpu.VMEM((ROWS, ROWS), F32),
            pltpu.VMEM((size // 2, ROWS), F32),
            pltpu.VMEM((size // 4, ROWS), F32),
            pltpu.VMEM((size // 4, ROWS), F32),
            pltpu.VMEM((chunks, N_X, STEP, WIDE), BF16),
            pltpu.VMEM((4 * STEP, ROWS), F32),
            pltpu.VMEM((EX_DEV, size, LEN), F32),
            pltpu.VMEM((8, ROWS), F32),
            pltpu.VMEM((8, LEN), F32),
            pltpu.VMEM((8, 8, LEN), F32),
            pltpu.VMEM((8, LEN), F32),
            pltpu.VMEM((8, LEN), F32),
            dma((2,)),
            dma((N_G,)),
            dma((N_G,)),
            dma((chunks,)),
            dma((chunks,)),
            dma((5,)),
            dma((5,)),
            dma((8,)),
            dma((9,)),
        ],
        compiler_params=pltpu.CompilerParams(
            collective_id=size // STEP, has_side_effects=True, vmem_limit_bytes=56 << 20
        ),
    )(lengths, far_len, blk, p1, gs, gk, ok, tl)


SIZES = (512,)


def on_device(activations, out_grads, lengths):
    ok, tl, gk, gs, p1, blk, far_len, most = run_first(lengths, activations[0], out_grads[0])
    needed = most[4, 0]
    branches = [functools.partial(run_second, size) for size in SIZES]
    args = (lengths, far_len, blk, p1, gs, gk, ok, tl)
    if len(branches) == 1:
        return branches[0](*args)
    which = sum((needed > size).astype(jnp.int32) for size in SIZES[:-1])
    return lax.switch(which, branches, *args)


def solution(mesh):
    placed = (P("section", "ex", "tp"), P("section", "ex", "tp"), P("ex"))
    return jax.shard_map(
        on_device,
        mesh=mesh,
        in_specs=placed,
        out_specs=(P("ex", None), P("ex", None)),
        check_vma=False,
    )
```

time: 235 us -> 138 us (0.59)
  waiting for transfers between devices: 169 us -> 0 us
  Pallas kernels: 0 us -> 135 us
  matrix products: 21.8 us -> 0 us
  starting transfers between devices: 17.5 us -> 0 us
  blocking collectives: 8.14 us -> 0 us
  local copies, waits for them, and re-layouts: 9.91 us -> 2.49 us
  other arithmetic: 6.96 us -> 0 us
    pallas_call x0 -> x2, Pallas kernels: none -> 135 us  [the longest x1 104 us: run_second(): pl.pallas_call(functools.partial(second_kernel, size), name='cross_part_%...]
    ppermute x5 -> x0, waiting for transfers between devices: 124 us -> none  [from_behind(): return lax.ppermute(value, axis, pairs)]
    all_to_all x1 -> x0, waiting for transfers between devices: 44.8 us -> none  [sent_and_summed(): lax.all_to_all(cut_along(shard, dim, peers), axis, 0, 0, tiled=True)]
    dot_general x8 -> x0, matrix products: 21.8 us -> none  [the longest x4 19.9 us: gram_of(): lax.dot_general(left, right, (((1,), (1,)), ((), ())), preferred_element_...]
    ppermute x5 -> x0, starting transfers between devices: 9.56 us -> none  [from_behind(): return lax.ppermute(value, axis, pairs)]
    all_to_all x1 -> x0, blocking collectives: 8.14 us -> none  [sent_to_all(): lax.all_to_all(jnp.broadcast_to(shard[None], (peers, *shard.shape)), axis...]
    all_to_all x1 -> x0, starting transfers between devices: 7.97 us -> none  [sent_and_summed(): lax.all_to_all(cut_along(shard, dim, peers), axis, 0, 0, tiled=True)]
    dynamic_slice x2 -> x0, local copies, waits for them, and re-layouts: 4.35 us -> none  [the longest x1 4.26 us: on_device(): lax.dynamic_slice_in_dim(feats, jnp.where(lower, half_x, 0).astype(jnp.in...]
  transfers between devices with their start and end apart: 6 -> 0, of which waited for: 5 -> 0; matrix products, arithmetic and copies ran while one was open for 11% -> 0% of each run, Pallas kernels for 0% -> 0%
where the time goes in v1:
time: 138 us
  Pallas kernels  135 us (98%)
  local copies, waits for them, and re-layouts  2.49 us (2%)
    pallas_call x1, Pallas kernels, run_second(): pl.pallas_call(functools.partial(second_kernel, size), name='cross_part_%...  104 us
    pallas_call x1, Pallas kernels, run_first(): pl.pallas_call(first_kernel, name='block_part', out_shape=(jax.ShapeDtype...  30.4 us

profile of v1, /device:TPU:1, one launch (start us, length us, event | category | flops | bytes accessed | tf_op | source)
XLA Modules:
  0.0 138.0 jit_solution(2549751813943810568)
XLA Ops:
  0.6 30.4 %block_part.1 = (bf16[7,512,512]{2,1,0:T(8,128)(2,1)}, bf16[7,384,512]{2,1,0:T(8,128)(2,1)}, bf16[2,512,512]{2,1,0:T(8,128)(2,1)}, bf16[2,512,512]{2,1,0:T(8,128...) custom-call(s32[4]{0:T(128)} %lens.3, bf16[512,7168]{1,0:T(8,128)(2,1)} %bitcast.2, ...), custom_call_target="tpu_custom_call" | custom-call | tf_op jit(solution)/shard_map/block_part/pallas_call | solution.py:452
  31.0 104.4 %cross_part_512.1 = (f32[4,4]{1,0:T(4,128)}, f32[4,4]{1,0:T(4,128)}) custom-call(s32[4]{0:T(128)} %lens.3, s32[8,128]{1,0:T(8,128)} %get-tuple-element.9.far_len, f32[8,128]{1,0:T(8,128)} %get-tuple-element.10.blk_ref, f32[128,512]{1,0:T(8,128)} %get-tuple-element.11.p1_ref, bf16[2,512,512]{2,1,0:T(8,128)(2,1)} %get-tuple-element.12.gs_hbm, ...), custom_call_target="tpu_custom_call" | custom-call | tf_op jit(solution)/shard_map/cross_part_512/pallas_call | solution.py:501
  135.5 1.2 copy.7
  136.7 1.2 copy.8

commit v2 on v1

v2 whole, which is shorter than its diff:
```python
import functools

import jax
import jax.numpy as jnp
from jax import lax
from jax.experimental import pallas as pl
from jax.experimental.pallas import tpu as pltpu
from jax.sharding import PartitionSpec as P

D = 8192
FF = 28672
LEN = 128
EX_DEV = 4
ROWS = EX_DEV * LEN
WIDE = 512
PANEL = 256
F_TP = 14
D_TP = 4
N_X = 14
N_G = 4
TURN = 288
EVENTS = (2, 6, 8)
SURE = 16
BASE = EX_DEV * SURE
DEPTH = 2
STEP = 32
SIZES = tuple(range(288, ROWS + 1, STEP))
MESH = pl.DeviceIdType.MESH
F32 = jnp.float32
BF16 = jnp.bfloat16


def dot_nt(left, right):
    return lax.dot_general(left, right, (((1,), (1,)), ((), ())), preferred_element_type=F32)


def place():
    s = lax.axis_index("section")
    e = lax.axis_index("ex")
    t = lax.axis_index("tp")
    return s, e, t


def remote(src, dst, send, recv, device):
    return pltpu.make_async_remote_copy(
        src_ref=src, dst_ref=dst, send_sem=send, recv_sem=recv, device_id=device, device_id_type=MESH
    )


def greet(peers):
    barrier = pltpu.get_barrier_semaphore()
    for peer in peers:
        pl.semaphore_signal(barrier, inc=1, device_id=peer, device_id_type=MESH)
    return lambda: pl.semaphore_wait(barrier, len(peers))


def iota(shape, dim):
    return lax.broadcasted_iota(jnp.int32, shape, dim)


def block_tiles(rows_ref, j, out_ref):
    at = 0
    for a in range(EX_DEV - 1):
        width = (EX_DEV - 1 - a) * LEN
        out_ref[:, at : at + width] += dot_nt(
            rows_ref[j, a * LEN : (a + 1) * LEN, :], rows_ref[j, (a + 1) * LEN :, :]
        )
        at += width


def first_kernel(
    lens, x_hbm, g_hbm,
    near_hbm, pick_ref, blk_ref, far_len_ref, which_ref,
    xraw, graw, near, xd, gd, r_core, r_z, r_back, lt, mt, lx, ly,
    ld_sem, out_sem, s_send, s_recv, d_send, d_recv, l_send, l_recv,
):
    s, e, t = place()
    x, y = e // 4, lax.rem(e, 4)
    hi = e // 8
    core, z = lax.rem(t, 2), t // 2
    partner = (s, lax.rem(e + 8, 16), t)
    core_peer = (s, e, t + 1 - 2 * core)
    z_peer = (s, e, lax.rem(t + 2, 4))
    x_peers = [(s, lax.rem(x + d, 4) * 4 + y, t) for d in (1, 2, 3)]
    y_peers = [(s, x * 4 + lax.rem(y + d, 4), t) for d in (1, 2, 3)]
    met = greet(x_peers + y_peers + [core_peer, z_peer])

    def load(ref, to, j, at):
        return pltpu.make_async_copy(ref.at[:, pl.ds(pl.multiple_of(j * WIDE, WIDE), WIDE)], to.at[j], ld_sem.at[at + j])

    for j in range(D_TP):
        load(g_hbm, graw, j, 0).start()
    for j in range(F_TP):
        load(x_hbm, xraw, j, D_TP).start()

    counts = [lens[j] for j in range(EX_DEV)]
    starts = [jnp.int32(BASE)]
    for j in range(EX_DEV):
        starts.append(starts[-1] + counts[j] - SURE)
    row = iota((8, LEN), 0)
    mine = jnp.full((8, LEN), starts[EX_DEV], jnp.int32)
    for j in range(EX_DEV):
        mine = jnp.where(row == j, counts[j], mine)
    lt[...] = mine
    met()
    for i, peer in enumerate(x_peers):
        remote(lt, lx.at[i], l_send.at[i], l_recv.at[i], peer).start()

    def send_x(j):
        rows = pl.ds(j * SURE, SURE)
        at = pl.multiple_of((1 - hi) * N_X * PANEL, PANEL)
        return remote(
            x_hbm.at[pl.ds(j * LEN, SURE), pl.ds(at, N_X * PANEL)], near.at[rows], s_send.at[j], s_recv.at[j], partner
        )

    for j in range(EX_DEV):
        send_x(j).start()
    xd[...] = jnp.zeros_like(xd)
    gd[...] = jnp.zeros_like(gd)

    def gram_g(j, carry):
        load(g_hbm, graw, j, 0).wait()
        block_tiles(graw, j, gd)
        return carry

    lax.fori_loop(0, D_TP, gram_g, 0)
    half = LEN // 2
    keep = pl.multiple_of(core * half, half)
    give = pl.multiple_of((1 - core) * half, half)
    to_core = remote(gd.at[pl.ds(give, half)], r_core, d_send.at[0], d_recv.at[0], core_peer)
    to_core.start()
    for b in range(EX_DEV):
        packed = iota((LEN, LEN), 0) + b * LEN
        source = jnp.full((LEN, LEN), -1, jnp.int32)
        for j in reversed(range(EX_DEV)):
            source = jnp.where(packed < starts[j + 1], packed - starts[j] + j * LEN + SURE, source)
        if b * LEN < BASE:
            source = jnp.where(packed < BASE, packed // SURE * LEN + lax.rem(packed, SURE), source)
        for c in range(EX_DEV):
            pick_ref[b * LEN : (b + 1) * LEN, c * LEN : (c + 1) * LEN] = jnp.where(
                source == iota((LEN, LEN), 1) + c * LEN, 1.0, 0.0
            ).astype(BF16)
    to_core.wait()
    gd[pl.ds(keep, half), :] += r_core[...]
    for i in range(3):
        remote(lt, lx.at[i], l_send.at[i], l_recv.at[i], x_peers[i]).wait_recv()
    mt[...] = jnp.maximum(jnp.maximum(lt[...], lx[0]), jnp.maximum(lx[1], lx[2]))
    far_len_ref[...] = lx[1]
    to_z = remote(gd.at[pl.ds(keep, half)], r_z, d_send.at[1], d_recv.at[1], z_peer)
    to_z.start()
    for i, peer in enumerate(y_peers):
        remote(mt, ly.at[i], l_send.at[3 + i], l_recv.at[3 + i], peer).start()

    def gram_x(j, carry):
        load(x_hbm, xraw, j, D_TP).wait()
        block_tiles(xraw, j, xd)
        return carry

    lax.fori_loop(0, F_TP, gram_x, 0)
    to_z.wait()
    gd[pl.ds(keep, half), :] += r_z[...]
    back = remote(gd.at[pl.ds(keep, half)], r_back, d_send.at[2], d_recv.at[2], core_peer)
    back.start()
    for i in range(3):
        remote(mt, ly.at[i], l_send.at[3 + i], l_recv.at[3 + i], y_peers[i]).wait_recv()
    most = jnp.maximum(jnp.maximum(mt[...], ly[0]), jnp.maximum(ly[1], ly[2]))
    which = jnp.zeros((8, LEN), jnp.int32)
    for size in SIZES[:-1]:
        which = which + jnp.where(most > size, 1, 0)
    which_ref[0] = jnp.max(which)
    back.wait()
    gd[pl.ds(give, half), :] = r_back[...]
    blk = jnp.zeros((8, LEN), F32)
    lane = iota((8, LEN), 1)
    inner_row = iota((LEN, LEN), 0)
    inner_lane = iota((LEN, LEN), 1)
    scale_x = 1.0 / jnp.sqrt(jnp.full((LEN, LEN), float(FF), F32))
    scale_g = 1.0 / jnp.sqrt(jnp.full((LEN, LEN), float(D), F32))
    inverse = [1.0 / jnp.sqrt(jnp.full((8, LEN), counts[j].astype(F32), F32)) for j in range(EX_DEV)]
    at = 0
    for a in range(EX_DEV - 1):
        for b in range(a + 1, EX_DEV):
            product = (xd[:, at : at + LEN] * scale_x) * (gd[:, at : at + LEN] * scale_g)
            live = (inner_row < counts[a]) & (inner_lane < counts[b])
            product = jnp.where(live, product, 0.0)
            total = jnp.sum(jnp.sum(product, axis=0, keepdims=True), axis=1, keepdims=True)
            spot = ((row == a) & (lane == 8 + b)) | ((row == b) & (lane == 8 + a))
            blk = blk + jnp.where(spot, jnp.broadcast_to(total, (8, LEN)) * inverse[a] * inverse[b], 0.0)
            at += LEN
    blk_ref[...] = blk
    for j in range(EX_DEV):
        send_x(j).wait()
    out = pltpu.make_async_copy(near, near_hbm, out_sem.at[0])
    out.start()
    for i in range(3):
        remote(lt, lx.at[i], l_send.at[i], l_recv.at[i], x_peers[i]).wait_send()
        remote(mt, ly.at[i], l_send.at[3 + i], l_recv.at[3 + i], y_peers[i]).wait_send()
    out.wait()


def second_kernel(
    size, lens, far_len_hbm, blk_hbm, pick_hbm, near_hbm, x_hbm, g_hbm,
    out_ref,
    xraw, graw, xs, xk, gs, gb, cp, cf, gg, r1, r2, r3, farx, prod, wl, acc, tile, gather, pick, far_len, blk_ref,
    in_sem, ld_sem, lx_sem, near_sem, g_send, g_recv, x_send, x_recv, r_send, r_recv, t_send, t_recv,
):
    s, e, t = place()
    hi = e // 8
    core, z = lax.rem(t, 2), t // 2
    partner = (s, lax.rem(e + 8, 16), t)
    core_peer = (s, e, t + 1 - 2 * core)
    z_peer = (s, e, lax.rem(t + 2, 4))
    me = s * 4 + t
    column = []
    for d in range(1, 8):
        other = lax.rem(me + d, 8)
        column.append((other // 4, e, lax.rem(other, 4)))
    met = greet([partner] + column)

    def load_g(j):
        half = jnp.where(j < N_G, 1 - hi, hi)
        at = pl.multiple_of((half * N_G + lax.rem(j, N_G)) * PANEL, PANEL)
        return pltpu.make_async_copy(g_hbm.at[:, pl.ds(at, PANEL)], graw.at[j], ld_sem.at[j])

    def load_x(j):
        half = jnp.where(j < N_X, 1 - hi, hi)
        at = pl.multiple_of((half * N_X + lax.rem(j, N_X)) * PANEL, PANEL)
        return pltpu.make_async_copy(x_hbm.at[:, pl.ds(at, PANEL)], xraw.at[j], lx_sem.at[j])

    def load_near(j):
        at = pl.multiple_of(j * PANEL, PANEL)
        return pltpu.make_async_copy(near_hbm.at[:, pl.ds(at, PANEL)], farx.at[j, pl.ds(0, BASE), :], near_sem.at[j])

    def each(count, fn):
        def body(j, carry):
            fn(j)
            return carry

        lax.fori_loop(0, count, body, 0)

    small = [
        pltpu.make_async_copy(pick_hbm, pick, in_sem.at[0]),
        pltpu.make_async_copy(far_len_hbm, far_len, in_sem.at[1]),
        pltpu.make_async_copy(blk_hbm, blk_ref, in_sem.at[2]),
    ]
    small[0].start()
    each(N_G, lambda j: load_g(j).start())
    for copy in small[1:]:
        copy.start()
    each(N_G, lambda j: load_g(N_G + j).start())
    each(2 * N_X, lambda j: load_x(j).start())
    each(N_X, lambda j: load_near(j).start())

    def packed(raw, to):
        top = min(size, TURN)
        to[0:top, :] = jnp.dot(pick[0:top, :], raw[...], preferred_element_type=F32).astype(BF16)
        if size > top:
            to[top:size, :] = jnp.dot(
                pick[top:size, ROWS // 2 :], raw[ROWS // 2 :, :], preferred_element_type=F32
            ).astype(BF16)

    def pack_g_sent(c):
        load_g(c).wait()
        packed(graw.at[c], gs.at[c])

    small[0].wait()
    each(N_G, pack_g_sent)
    for copy in small[1:]:
        copy.wait()
    met()

    def send_g(c):
        return remote(
            gs.at[c], gb.at[1 - hi, c, pl.ds(0, size), :], g_send.at[c], g_recv.at[c], partner
        )

    def got_g(c):
        return remote(
            gs.at[c], gb.at[hi, c, pl.ds(0, size), :], g_send.at[c], g_recv.at[c], partner
        )

    def send_x(c):
        rows = pl.ds(BASE, size - BASE)
        return remote(xs.at[c, rows, :], farx.at[c, rows, :], x_send.at[c], x_recv.at[c], partner)

    each(N_G, lambda c: send_g(c).start())

    def pack_x_sent(c):
        load_x(c).wait()
        packed(xraw.at[c], xs.at[c])

    each(DEPTH + 1, pack_x_sent)
    for c in range(DEPTH):
        send_x(c).start()

    if size < ROWS:
        gb[:, :, size:, :] = jnp.zeros((2, N_G, ROWS - size, PANEL), BF16)
        xk[:, size:, :] = jnp.zeros((N_X, ROWS - size, PANEL), BF16)
        cf[size:, :] = jnp.zeros((ROWS - size, ROWS), F32)

    def pack_g_kept(c):
        load_g(N_G + c).wait()
        packed(graw.at[N_G + c], gb.at[1 - hi, c])

    each(N_G, pack_g_kept)

    def pack_x_rest(c, carry):
        pack_x_sent(c)
        return carry

    lax.fori_loop(DEPTH + 1, N_X, pack_x_rest, 0)

    def pack_x_kept(c):
        load_x(N_X + c).wait()
        packed(xraw.at[N_X + c], xk.at[c])

    each(N_X, pack_x_kept)
    prod[...] = jnp.zeros_like(prod)
    acc[...] = jnp.zeros_like(acc)
    begin = jnp.full((1, LEN), BASE, jnp.int32)
    for a in range(EX_DEV):
        count = far_len[a : a + 1, :]
        inverse = 1.0 / jnp.sqrt(count.astype(F32))
        rows = iota((size, LEN), 0)
        end = begin + count - SURE
        sure = (rows >= a * SURE) & (rows < (a + 1) * SURE)
        wl[a] = jnp.where(sure | ((rows >= begin) & (rows < end)), inverse, 0.0)
        begin = end
    each(N_X, lambda j: load_near(j).wait())
    each(N_G, lambda c: got_g(c).wait_recv())
    half, quarter = size // 2, size // 4
    cp[...] = jnp.zeros_like(cp)

    def gram_g(c):
        cp[...] += dot_nt(gb[0, c, 0:size, :], gb[1, c])

    each(N_G, gram_g)
    keep_half = pl.multiple_of(core * half, 8)
    give_half = pl.multiple_of((1 - core) * half, 8)
    keep = pl.multiple_of(core * half + z * quarter, 8)
    give = pl.multiple_of(core * half + (1 - z) * quarter, 8)

    step = remote(cp.at[pl.ds(give_half, half)], r1, r_send.at[0], r_recv.at[0], core_peer)
    step.start()
    step.wait()
    cp[pl.ds(keep_half, half), :] += r1[...]
    to_z = remote(cp.at[pl.ds(give, quarter)], r2, r_send.at[1], r_recv.at[1], z_peer)
    to_z.start()

    def take(c):
        send_x(c).wait()

        @pl.when(c + DEPTH < N_X)
        def _():
            send_x(c + DEPTH).start()

        prod[...] += dot_nt(farx[c], xk[c])

    def take_from(first, last):
        def body(c, carry):
            take(c)
            return carry

        lax.fori_loop(first, last, body, 0)

    take_from(0, EVENTS[0])
    to_z.wait()
    cp[pl.ds(keep, quarter), :] += r2[...]
    to_x = remote(cp.at[pl.ds(keep, quarter)], r3, r_send.at[2], r_recv.at[2], partner)
    to_x.start()
    take_from(EVENTS[0], EVENTS[1])
    to_x.wait()
    cf[pl.ds(keep, quarter), :] = cp[pl.ds(keep, quarter), :] + r3[...]
    back = remote(cf.at[pl.ds(keep, quarter)], cf.at[pl.ds(keep, quarter)], r_send.at[3], r_recv.at[3], z_peer)
    back.start()
    take_from(EVENTS[1], EVENTS[2])
    back.wait_send()
    remote(cf.at[pl.ds(keep, quarter)], cf.at[pl.ds(give, quarter)], r_send.at[3], r_recv.at[3], z_peer).wait_recv()
    back = remote(cf.at[pl.ds(keep_half, half)], cf.at[pl.ds(keep_half, half)], r_send.at[4], r_recv.at[4], core_peer)
    back.start()
    back.wait_send()
    remote(
        cf.at[pl.ds(keep_half, half)], cf.at[pl.ds(give_half, half)], r_send.at[4], r_recv.at[4], core_peer
    ).wait_recv()
    scale_g = 1.0 / jnp.sqrt(jnp.full((LEN, ROWS), float(D), F32))

    @pl.when(hi == 0)
    def _():
        for i in range(EX_DEV):
            gg[i * LEN : (i + 1) * LEN, :] = cf[i * LEN : (i + 1) * LEN, :] * scale_g

    @pl.when(hi == 1)
    def _():
        for i in range(EX_DEV):
            for j in range(EX_DEV):
                turned = jnp.transpose(cf[j * LEN : (j + 1) * LEN, i * LEN : (i + 1) * LEN])
                gg[i * LEN : (i + 1) * LEN, j * LEN : (j + 1) * LEN] = turned * scale_g[:, :LEN]

    take_from(EVENTS[2], N_X)
    scale_x = 1.0 / jnp.sqrt(jnp.full((STEP, LEN), float(FF), F32))

    def weigh(i):
        rows = pl.ds(pl.multiple_of(i * STEP, STEP), STEP)
        for b in range(EX_DEV):
            lanes = slice(b * LEN, (b + 1) * LEN)
            product = (prod[rows, lanes] * scale_x) * gg[rows, lanes]
            for a in range(EX_DEV):
                acc[a : a + 1, lanes] += jnp.sum(product * wl[a, rows, :], axis=0, keepdims=True)

    each(size // STEP, weigh)
    lane = iota((8, LEN), 1)
    wide_row, wide_lane = iota((8, ROWS), 0), iota((8, ROWS), 1)
    right = jnp.zeros((8, ROWS), F32)
    begin = jnp.int32(BASE)
    for b in range(EX_DEV):
        count = lens[b]
        inverse = 1.0 / jnp.sqrt(jnp.full((8, ROWS), count.astype(F32), F32))
        end = begin + count - SURE
        sure = (wide_lane >= b * SURE) & (wide_lane < (b + 1) * SURE)
        inside = (wide_row == b) & (sure | ((wide_lane >= begin) & (wide_lane < end)))
        right = jnp.where(inside, inverse, right)
        begin = end
    found = acc[...]
    out = blk_ref[...]
    for a in range(EX_DEV):
        summed = jnp.sum(right * found[a : a + 1, :], axis=1, keepdims=True)
        out = out + jnp.where(lane == a, summed, 0.0)
        summed = jnp.sum(found * right[a : a + 1, :], axis=1, keepdims=True)
        out = out + jnp.where(lane == 4 + a, summed, 0.0)
    tile[...] = out
    mine = hi * 8 + me

    def tell(i):
        to = lax.rem(mine + i, 16)
        other = lax.rem(to, 8)
        side = to // 8
        device = (other // 4, lax.rem(e, 8) + 8 * side, lax.rem(other, 4))
        return remote(tile, gather.at[mine], t_send.at[i], t_recv.at[mine], device)

    for i in range(1, 16):
        tell(i).start()
    gather[mine] = out
    for i in range(1, 16):
        came = lax.rem(mine + i, 16)
        remote(tile, gather.at[came], t_send.at[i], t_recv.at[came], partner).wait_recv()
    whole = gather[8 * hi]
    across = gather[8 - 8 * hi]
    for i in range(1, 8):
        whole = whole + gather[8 * hi + i]
        across = across + gather[8 - 8 * hi + i]
    out_ref[:, 0:4] = whole[:4, 0:4] + across[:4, 4:8]
    out_ref[:, 4:8] = whole[:4, 8:12]
    for i in range(1, 16):
        tell(i).wait_send()
    each(N_G, lambda c: send_g(c).wait_send())


def vmem():
    return pl.BlockSpec(memory_space=pltpu.VMEM)


def hbm():
    return pl.BlockSpec(memory_space=pl.ANY)


def smem():
    return pl.BlockSpec(memory_space=pltpu.SMEM)


def run_first(lengths, feats, grads):
    dma = pltpu.SemaphoreType.DMA
    return pl.pallas_call(
        first_kernel,
        name="block_part",
        out_shape=(
            jax.ShapeDtypeStruct((BASE, N_X * PANEL), BF16),
            jax.ShapeDtypeStruct((ROWS, ROWS), BF16),
            jax.ShapeDtypeStruct((8, LEN), F32),
            jax.ShapeDtypeStruct((8, LEN), jnp.int32),
            jax.ShapeDtypeStruct((1,), jnp.int32),
        ),
        in_specs=[smem(), hbm(), hbm()],
        out_specs=(hbm(), vmem(), vmem(), vmem(), smem()),
        scratch_shapes=[
            pltpu.VMEM((F_TP, ROWS, WIDE), BF16),
            pltpu.VMEM((D_TP, ROWS, WIDE), BF16),
            pltpu.VMEM((BASE, N_X * PANEL), BF16),
            pltpu.VMEM((LEN, 6 * LEN), F32),
            pltpu.VMEM((LEN, 6 * LEN), F32),
            pltpu.VMEM((LEN // 2, 6 * LEN), F32),
            pltpu.VMEM((LEN // 2, 6 * LEN), F32),
            pltpu.VMEM((LEN // 2, 6 * LEN), F32),
            pltpu.VMEM((8, LEN), jnp.int32),
            pltpu.VMEM((8, LEN), jnp.int32),
            pltpu.VMEM((3, 8, LEN), jnp.int32),
            pltpu.VMEM((3, 8, LEN), jnp.int32),
            dma((F_TP + D_TP,)),
            dma((1,)),
            dma((EX_DEV,)),
            dma((EX_DEV,)),
            dma((3,)),
            dma((3,)),
            dma((6,)),
            dma((6,)),
        ],
        compiler_params=pltpu.CompilerParams(collective_id=0, has_side_effects=True, vmem_limit_bytes=56 << 20),
    )(lengths, feats, grads)


def run_second(size, lengths, far_len, blk, pick, near, feats, grads):
    dma = pltpu.SemaphoreType.DMA
    return pl.pallas_call(
        functools.partial(second_kernel, size),
        name="cross_part_%d" % size,
        out_shape=jax.ShapeDtypeStruct((4, 8), F32),
        in_specs=[smem()] + [hbm()] * 6,
        out_specs=vmem(),
        scratch_shapes=[
            pltpu.VMEM((2 * N_X, ROWS, PANEL), BF16),
            pltpu.VMEM((2 * N_G, ROWS, PANEL), BF16),
            pltpu.VMEM((N_X, size, PANEL), BF16),
            pltpu.VMEM((N_X, ROWS, PANEL), BF16),
            pltpu.VMEM((N_G, size, PANEL), BF16),
            pltpu.VMEM((2, N_G, ROWS, PANEL), BF16),
            pltpu.VMEM((size, ROWS), F32),
            pltpu.VMEM((ROWS, ROWS), F32),
            pltpu.VMEM((ROWS, ROWS), F32),
            pltpu.VMEM((size // 2, ROWS), F32),
            pltpu.VMEM((size // 4, ROWS), F32),
            pltpu.VMEM((size // 4, ROWS), F32),
            pltpu.VMEM((N_X, size, PANEL), BF16),
            pltpu.VMEM((size, ROWS), F32),
            pltpu.VMEM((EX_DEV, size, LEN), F32),
            pltpu.VMEM((8, ROWS), F32),
            pltpu.VMEM((8, LEN), F32),
            pltpu.VMEM((16, 8, LEN), F32),
            pltpu.VMEM((ROWS, ROWS), BF16),
            pltpu.VMEM((8, LEN), jnp.int32),
            pltpu.VMEM((8, LEN), F32),
            dma((3,)),
            dma((2 * N_G,)),
            dma((2 * N_X,)),
            dma((N_X,)),
            dma((N_G,)),
            dma((N_G,)),
            dma((N_X,)),
            dma((N_X,)),
            dma((5,)),
            dma((5,)),
            dma((16,)),
            dma((16,)),
        ],
        compiler_params=pltpu.CompilerParams(
            collective_id=size // STEP, has_side_effects=True, vmem_limit_bytes=56 << 20
        ),
    )(lengths, far_len, blk, pick, near, feats, grads)


def on_device(activations, out_grads, lengths):
    feats, grads = activations[0], out_grads[0]
    near, pick, blk, far_len, which = run_first(lengths, feats, grads)
    branches = [functools.partial(run_second, size) for size in SIZES]
    out = lax.switch(which[0], branches, lengths, far_len, blk, pick, near, feats, grads)
    return out[:, 4:8], out[:, 0:4]


def solution(mesh):
    placed = (P("section", "ex", "tp"), P("section", "ex", "tp"), P("ex"))
    return jax.shard_map(
        on_device,
        mesh=mesh,
        in_specs=placed,
        out_specs=(P("ex", None), P("ex", None)),
        check_vma=False,
    )
```

time: 138 us -> 115 us (0.83)
  Pallas kernels: 135 us -> 112 us
    pallas_call x1, Pallas kernels: 104 us -> 91.6 us  [run_second(): pl.pallas_call(functools.partial(second_kernel, size), name='cross_part_%...]
    pallas_call x1, Pallas kernels: 30.4 us -> 20.4 us  [run_first(): pl.pallas_call(first_kernel, name='block_part', out_shape=(jax.ShapeDtype...]
    unnamed x2, local copies, waits for them, and re-layouts: 2.49 us -> 0.01 us
where the time goes in v2:
time: 115 us
  Pallas kernels  112 us (97%)
  local copies, waits for them, and re-layouts  1.38 us (1%)
  between operations  1.22 us (1%)
    pallas_call x1, Pallas kernels, run_second(): pl.pallas_call(functools.partial(second_kernel, size), name='cross_part_%...  91.6 us
    pallas_call x1, Pallas kernels, run_first(): pl.pallas_call(first_kernel, name='block_part', out_shape=(jax.ShapeDtype...  20.4 us

profile of v2, /device:TPU:1, one launch (start us, length us, event | category | flops | bytes accessed | tf_op | source)
XLA Modules:
  0.0 115.2 jit_solution(9398991912402928938)
XLA Ops:
  0.6 0.0 copy-start
  0.6 20.4 %block_part.1 = (bf16[64,3584]{1,0:T(8,128)(2,1)S(1)}, bf16[512,512]{1,0:T(8,128)(2,1)S(1)}, f32[8,128]{1,0:T(8,128)}, s32[8,128]{1,0:T(8,128)}, s32[1]{0:T(128)}) custom-call(s32[4]{0:T(128)} %lens.1, bf16[512,7168]{1,0:T(8,128)(2,1)} %bitcast.3, bf16[512,2048]{1,0:T(8,128)(2,1)} %bitcast.12), custom_call_target="tpu_custom_call" | custom-call | tf_op jit(solution)/shard_map/block_part/pallas_call | solution.py:472
  21.6 0.0 copy-done
  21.6 92.2 %conditional.1 = (f32[4,8]{1,0:T(4,128)}) conditional(s32[]{:T(128)} %bitcast.2, (s32[4]{0:T(128)}, s32[8,128]{1,0:T(8,128)}, f32[8,128]{1,0:T(8,128)}, bf16[512,512]{1,0:T(8,128)(2,1)S(1)}, bf16[64,3584]{1,0:T(8,128)(2,1)S(1)}, /*index=5*/bf16[512,7168]{1,0:T(8,128)(2,1)S(1)}, ...), branch_computations={%region_0.0_spmd, %region_1.0_spmd, %region_2.0_spmd, %region_3.0_... | conditional | bytes 8 | solution.py:563
  21.9 91.6 %cross_part_416.1 = f32[4,8]{1,0:T(4,128)} custom-call(s32[4]{0:T(128)} %get-tuple-element.149.lens, s32[8,128]{1,0:T(8,128)} %get-tuple-element.150.far_len_hbm, f32[8,128]{1,0:T(8,128)} %get-tuple-element.151.blk_hbm, bf16[512,512]{1,0:T(8,128)(2,1)S(1)} %get-tuple-element.152.pick_hbm, bf16[64,3584]{1,0:T(8,128)(2,1)S(1)} %get-tuple-element.153.near_hbm, ...), custom_call_target="tpu_custom_call" | custom-call | tf_op jit(solution)/shard_map/cond/branch_4_fun/cross_part_416/pallas_call | solution.py:512
  113.8 1.4 %fusion = (f32[4,4]{1,0:T(4,128)}, f32[4,4]{1,0:T(4,128)}) fusion(f32[4,8]{1,0:T(4,128)} %get-tuple-element.191), kind=kLoop, calls=%fused_computation | loop fusion | bytes 256 | tf_op jit(solution)/shard_map/slice | solution.py:564
Async XLA Ops:
  0.6 21.0 %copy-start = (bf16[1,512,7168]{2,1,0:T(8,128)(2,1)S(1)}, bf16[1,512,7168]{2,1,0:T(8,128)(2,1)}, u32[]{:S(2)}) copy-start(bf16[1,512,7168]{2,1,0:T(8,128)(2,1)} %param.11) | copy-start | bytes 22020100

commit v3 on v2

--- a/solution.py
+++ b/solution.py
@@ -14,17 +14,29 @@
 ROWS = EX_DEV * LEN
 WIDE = 512
 PANEL = 256
+NARROW = 128
 F_TP = 14
 D_TP = 4
-N_X = 14
-N_G = 4
-TURN = 288
-EVENTS = (2, 6, 8)
+X_PANELS = 28
+G_PANELS = 16
 SURE = 16
 BASE = EX_DEV * SURE
-DEPTH = 2
-STEP = 32
-SIZES = tuple(range(288, ROWS + 1, STEP))
+SURE_PANELS = 10
+CHUNKS = 14
+G_CHUNKS = 2
+DEPTH = 3
+TURN = 288
+EVENTS = (1, 6, 9)
+VARIANTS = (
+    (400, 304),
+    (416, 320),
+    (400, 352),
+    (448, 336),
+    (464, 352),
+    (448, 384),
+    (480, 416),
+    (512, 512),
+)
 MESH = pl.DeviceIdType.MESH
 F32 = jnp.float32
 BF16 = jnp.bfloat16
@@ -108,10 +120,9 @@
 
     def send_x(j):
         rows = pl.ds(j * SURE, SURE)
-        at = pl.multiple_of((1 - hi) * N_X * PANEL, PANEL)
-        return remote(
-            x_hbm.at[pl.ds(j * LEN, SURE), pl.ds(at, N_X * PANEL)], near.at[rows], s_send.at[j], s_recv.at[j], partner
-        )
+        at = pl.multiple_of(hi * (X_PANELS - SURE_PANELS) * PANEL, PANEL)
+        source = x_hbm.at[pl.ds(j * LEN, SURE), pl.ds(at, SURE_PANELS * PANEL)]
+        return remote(source, near.at[rows], s_send.at[j], s_recv.at[j], partner)
 
     for j in range(EX_DEV):
         send_x(j).start()
@@ -144,7 +155,9 @@
     gd[pl.ds(keep, half), :] += r_core[...]
     for i in range(3):
         remote(lt, lx.at[i], l_send.at[i], l_recv.at[i], x_peers[i]).wait_recv()
-    mt[...] = jnp.maximum(jnp.maximum(lt[...], lx[0]), jnp.maximum(lx[1], lx[2]))
+    smaller = jnp.maximum(jnp.minimum(lt[...], lx[1]), jnp.minimum(lx[0], lx[2]))
+    larger = jnp.maximum(jnp.maximum(lt[...], lx[0]), jnp.maximum(lx[1], lx[2]))
+    mt[...] = jnp.where(row == 5, smaller, larger)
     far_len_ref[...] = lx[1]
     to_z = remote(gd.at[pl.ds(keep, half)], r_z, d_send.at[1], d_recv.at[1], z_peer)
     to_z.start()
@@ -164,9 +177,10 @@
     for i in range(3):
         remote(mt, ly.at[i], l_send.at[3 + i], l_recv.at[3 + i], y_peers[i]).wait_recv()
     most = jnp.maximum(jnp.maximum(mt[...], ly[0]), jnp.maximum(ly[1], ly[2]))
-    which = jnp.zeros((8, LEN), jnp.int32)
-    for size in SIZES[:-1]:
-        which = which + jnp.where(most > size, 1, 0)
+    which = jnp.full((1, LEN), len(VARIANTS) - 1, jnp.int32)
+    for i in reversed(range(len(VARIANTS) - 1)):
+        fits = (most[4:5, :] <= VARIANTS[i][0]) & (most[5:6, :] <= VARIANTS[i][1])
+        which = jnp.where(fits, i, which)
     which_ref[0] = jnp.max(which)
     back.wait()
     gd[pl.ds(give, half), :] = r_back[...]
@@ -198,12 +212,49 @@
     out.wait()
 
 
+def up(value, step):
+    return -(-value // step) * step
+
+
+class Plan:
+    def __init__(self, large, small):
+        self.large, self.small = large, small
+        self.grid = up(large, 32)
+        c = min(range(SURE_PANELS, X_PANELS // 2 + 1), key=lambda c: max(c * large, (X_PANELS - c) * small))
+        d = min(range(1, G_PANELS // 2 + 1), key=lambda d: max(d * large, (G_PANELS - d) * small))
+        self.g_panels = (d, G_PANELS - d)
+        self.x_panels = (c, X_PANELS - c)
+        self.rows = (large, small)
+        ends = [self.offset(r, n) for r, n in zip(self.rows, self.x_panels)]
+        self.chunk = up(up(max(ends), 16) // 16, CHUNKS) // CHUNKS * 16
+        g_ends = [r * n for r, n in zip(self.rows, self.g_panels)]
+        self.g_chunk = up(max(g_ends) // 16, G_CHUNKS) // G_CHUNKS * 16
+
+    def offset(self, rows, panel):
+        return panel * rows - BASE * min(panel, SURE_PANELS)
+
+
+def pieces(total, bounds_a, bounds_b):
+    cuts = sorted({0, total} | {b for b in bounds_a + bounds_b if b < total})
+    return list(zip(cuts, cuts[1:]))
+
+
+def spot(bounds, first, at):
+    panel = 0
+    while panel + 1 < len(bounds) and bounds[panel + 1] <= at:
+        panel += 1
+    return panel, first[panel] + at - bounds[panel]
+
+
 def second_kernel(
-    size, lens, far_len_hbm, blk_hbm, pick_hbm, near_hbm, x_hbm, g_hbm,
+    plan, lens, far_len_hbm, blk_hbm, pick_hbm, near_hbm, x_hbm, g_hbm,
     out_ref,
-    xraw, graw, xs, xk, gs, gb, cp, cf, gg, r1, r2, r3, farx, prod, wl, acc, tile, gather, pick, far_len, blk_ref,
+    xraw, graw, xp, gp, sx, sg, fx, fg, nr, cp, cf, gg, r1, r2, r3, prod_l, prod_s, gram_l, gram_s,
+    wl, acc, tile, gather, pick, far_len, blk_ref,
     in_sem, ld_sem, lx_sem, near_sem, g_send, g_recv, x_send, x_recv, r_send, r_recv, t_send, t_recv,
 ):
+    large, small = plan.rows
+    size = large
     s, e, t = place()
     hi = e // 8
     core, z = lax.rem(t, 2), t // 2
@@ -218,105 +269,130 @@
     met = greet([partner] + column)
 
     def load_g(j):
-        half = jnp.where(j < N_G, 1 - hi, hi)
-        at = pl.multiple_of((half * N_G + lax.rem(j, N_G)) * PANEL, PANEL)
-        return pltpu.make_async_copy(g_hbm.at[:, pl.ds(at, PANEL)], graw.at[j], ld_sem.at[j])
+        at = pl.multiple_of(jnp.where(hi == 0, j, G_PANELS - 1 - j) * NARROW, NARROW)
+        to = graw.at[j // 2, :, pl.ds(pl.multiple_of(lax.rem(j, 2) * NARROW, NARROW), NARROW)]
+        return pltpu.make_async_copy(g_hbm.at[:, pl.ds(at, NARROW)], to, ld_sem.at[j])
 
     def load_x(j):
-        half = jnp.where(j < N_X, 1 - hi, hi)
-        at = pl.multiple_of((half * N_X + lax.rem(j, N_X)) * PANEL, PANEL)
+        at = pl.multiple_of(jnp.where(hi == 0, j, X_PANELS - 1 - j) * PANEL, PANEL)
         return pltpu.make_async_copy(x_hbm.at[:, pl.ds(at, PANEL)], xraw.at[j], lx_sem.at[j])
 
     def load_near(j):
-        at = pl.multiple_of(j * PANEL, PANEL)
-        return pltpu.make_async_copy(near_hbm.at[:, pl.ds(at, PANEL)], farx.at[j, pl.ds(0, BASE), :], near_sem.at[j])
-
-    def each(count, fn):
+        at = pl.multiple_of(jnp.where(hi == 0, SURE_PANELS - 1 - j, j) * PANEL, PANEL)
+        return pltpu.make_async_copy(near_hbm.at[:, pl.ds(at, PANEL)], nr.at[j], near_sem.at[j])
+
+    def each(first, last, fn):
         def body(j, carry):
             fn(j)
             return carry
 
-        lax.fori_loop(0, count, body, 0)
-
-    small = [
+        lax.fori_loop(first, last, body, 0)
+
+    loads = [
         pltpu.make_async_copy(pick_hbm, pick, in_sem.at[0]),
         pltpu.make_async_copy(far_len_hbm, far_len, in_sem.at[1]),
         pltpu.make_async_copy(blk_hbm, blk_ref, in_sem.at[2]),
     ]
-    small[0].start()
-    each(N_G, lambda j: load_g(j).start())
-    for copy in small[1:]:
+    for copy in loads:
         copy.start()
-    each(N_G, lambda j: load_g(N_G + j).start())
-    each(2 * N_X, lambda j: load_x(j).start())
-    each(N_X, lambda j: load_near(j).start())
-
-    def packed(raw, to):
+    each(0, G_PANELS, lambda j: load_g(j).start())
+    each(0, X_PANELS, lambda j: load_x(j).start())
+    each(0, SURE_PANELS, lambda j: load_near(j).start())
+
+    def packed(raw, put):
         top = min(size, TURN)
-        to[0:top, :] = jnp.dot(pick[0:top, :], raw[...], preferred_element_type=F32).astype(BF16)
-        if size > top:
-            to[top:size, :] = jnp.dot(
-                pick[top:size, ROWS // 2 :], raw[ROWS // 2 :, :], preferred_element_type=F32
-            ).astype(BF16)
-
-    def pack_g_sent(c):
-        load_g(c).wait()
-        packed(graw.at[c], gs.at[c])
-
-    small[0].wait()
-    each(N_G, pack_g_sent)
-    for copy in small[1:]:
+        put(slice(0, top), jnp.dot(pick[0:top, :], raw[...], preferred_element_type=F32).astype(BF16))
+        rest = jnp.dot(pick[top:size, ROWS // 2 :], raw[ROWS // 2 :, :], preferred_element_type=F32)
+        put(slice(top, size), rest.astype(BF16))
+
+    def pack_g(c):
+        load_g(2 * c).wait()
+        load_g(2 * c + 1).wait()
+
+        def put(rows, value):
+            gp[2 * c, rows, :] = value[:, :NARROW]
+            gp[2 * c + 1, rows, :] = value[:, NARROW:]
+
+        packed(graw.at[c], put)
+
+    def pack_x(c):
+        load_x(c).wait()
+
+        def put(rows, value):
+            xp[c, rows, :] = value
+
+        packed(xraw.at[c], put)
+
+    for copy in loads:
         copy.wait()
+    own_total = lens[0] + lens[1] + lens[2] + lens[3]
+    far_total = jnp.max(far_len[...])
+    is_large = (own_total > far_total) | ((own_total == far_total) & (hi == 0))
+
+    def fill(to, source, chunk, count, bounds, first):
+        for a, b in pieces(chunk * count, *bounds):
+            (pa, ra), (pb, rb) = spot(bounds[0], first[0], a), spot(bounds[1], first[1], a)
+            if ra + b - a > large:
+                pa, ra = pb, rb
+            if rb + b - a > large:
+                pb, rb = pa, ra
+            if ra + b - a > large:
+                pa, ra, pb, rb = 0, 0, 0, 0
+            to[a:b, :] = lax.select_n(is_large, source[pb, rb : rb + b - a, :], source[pa, ra : ra + b - a, :])
+
+    def send_g(c):
+        rows = pl.ds(pl.multiple_of(c * plan.g_chunk, 16), plan.g_chunk)
+        return remote(sg.at[rows], fg.at[rows], g_send.at[c], g_recv.at[c], partner)
+
+    def send_x(c):
+        rows = pl.ds(pl.multiple_of(c * plan.chunk, 16), plan.chunk)
+        return remote(sx.at[rows], fx.at[rows], x_send.at[c], x_recv.at[c], partner)
+
+    g_bounds = [[p * r for p in range(n + 1)] for r, n in zip(plan.rows, plan.g_panels)]
+    x_bounds = [[plan.offset(r, p) for p in range(n + 1)] for r, n in zip(plan.rows, plan.x_panels)]
+    x_first = [[BASE if p < SURE_PANELS else 0 for p in range(len(b))] for b in x_bounds]
+    first_g = up(plan.g_panels[1], 2) // 2
+    each(0, first_g, pack_g)
+    fill(sg, gp, plan.g_chunk, G_CHUNKS, g_bounds, [[0] * len(b) for b in g_bounds])
     met()
-
-    def send_g(c):
-        return remote(
-            gs.at[c], gb.at[1 - hi, c, pl.ds(0, size), :], g_send.at[c], g_recv.at[c], partner
-        )
-
-    def got_g(c):
-        return remote(
-            gs.at[c], gb.at[hi, c, pl.ds(0, size), :], g_send.at[c], g_recv.at[c], partner
-        )
-
-    def send_x(c):
-        rows = pl.ds(BASE, size - BASE)
-        return remote(xs.at[c, rows, :], farx.at[c, rows, :], x_send.at[c], x_recv.at[c], partner)
-
-    each(N_G, lambda c: send_g(c).start())
-
-    def pack_x_sent(c):
-        load_x(c).wait()
-        packed(xraw.at[c], xs.at[c])
-
-    each(DEPTH + 1, pack_x_sent)
-    for c in range(DEPTH):
-        send_x(c).start()
-
+    each(0, G_CHUNKS, lambda k: send_g(k).start())
+    each(first_g, G_PANELS // 2, pack_g)
+
+    def all_x(c):
+        pack_x(c)
+
+        @pl.when(c == plan.x_panels[1] - 1)
+        def _():
+            fill(sx, xp, plan.chunk, CHUNKS, x_bounds, x_first)
+            each(0, DEPTH, lambda k: send_x(k).start())
+
+    each(0, X_PANELS, all_x)
     if size < ROWS:
-        gb[:, :, size:, :] = jnp.zeros((2, N_G, ROWS - size, PANEL), BF16)
-        xk[:, size:, :] = jnp.zeros((N_X, ROWS - size, PANEL), BF16)
+
+        def clear_g(p):
+            gp[p, size:, :] = jnp.zeros((ROWS - size, NARROW), BF16)
+
+        def clear_x(p):
+            xp[p, size:, :] = jnp.zeros((ROWS - size, PANEL), BF16)
+
+        each(0, G_PANELS, clear_g)
+        each(0, X_PANELS, clear_x)
+        cp[size:, :] = jnp.zeros((ROWS - size, ROWS), F32)
         cf[size:, :] = jnp.zeros((ROWS - size, ROWS), F32)
-
-    def pack_g_kept(c):
-        load_g(N_G + c).wait()
-        packed(graw.at[N_G + c], gb.at[1 - hi, c])
-
-    each(N_G, pack_g_kept)
-
-    def pack_x_rest(c, carry):
-        pack_x_sent(c)
-        return carry
-
-    lax.fori_loop(DEPTH + 1, N_X, pack_x_rest, 0)
-
-    def pack_x_kept(c):
-        load_x(N_X + c).wait()
-        packed(xraw.at[N_X + c], xk.at[c])
-
-    each(N_X, pack_x_kept)
-    prod[...] = jnp.zeros_like(prod)
     acc[...] = jnp.zeros_like(acc)
+    each(0, SURE_PANELS, lambda j: load_near(j).wait())
+    def clear(i):
+        rows = pl.ds(pl.multiple_of(i * 16, 16), 16)
+        for ref in (prod_s, prod_l, gram_s, gram_l):
+            ref[rows, :] = jnp.zeros((16, ROWS), F32)
+
+    each(0, size // 16, clear)
+
+    def near_part(p):
+        prod_s[0:BASE, :] += dot_nt(nr[p], xp[X_PANELS - 1 - p])
+
+    each(0, SURE_PANELS, near_part)
+    prod_l[0:BASE, :] = prod_s[0:BASE, :]
     begin = jnp.full((1, LEN), BASE, jnp.int32)
     for a in range(EX_DEV):
         count = far_len[a : a + 1, :]
@@ -326,15 +402,35 @@
         sure = (rows >= a * SURE) & (rows < (a + 1) * SURE)
         wl[a] = jnp.where(sure | ((rows >= begin) & (rows < end)), inverse, 0.0)
         begin = end
-    each(N_X, lambda j: load_near(j).wait())
-    each(N_G, lambda c: got_g(c).wait_recv())
-    half, quarter = size // 2, size // 4
-    cp[...] = jnp.zeros_like(cp)
-
-    def gram_g(c):
-        cp[...] += dot_nt(gb[0, c, 0:size, :], gb[1, c])
-
-    each(N_G, gram_g)
+    each(0, G_CHUNKS, lambda c: send_g(c).wait_recv())
+    half, quarter = plan.grid // 2, plan.grid // 4
+    for rows, count, to in ((small, plan.g_panels[1], gram_l), (large, plan.g_panels[0], gram_s)):
+
+        def gram_part(p, rows=rows, to=to):
+            at = pl.multiple_of(p * rows, 16)
+            to[0:rows, :] += dot_nt(fg[pl.ds(at, rows), :], gp[G_PANELS - 1 - p])
+
+        each(0, count, gram_part)
+
+    def spans(i):
+        i, j = i // EX_DEV, lax.rem(i, EX_DEV)
+        return pl.ds(pl.multiple_of(i * LEN, LEN), LEN), pl.ds(pl.multiple_of(j * LEN, LEN), LEN)
+
+    def turn(i, source, to):
+        rows, lanes = spans(i)
+        to[rows, lanes] = jnp.transpose(source[lanes, rows])
+
+    @pl.when(hi == 0)
+    def _():
+        cp[0:size, :] = lax.select_n(is_large, gram_s[...], gram_l[...])
+
+    @pl.when(hi == 1)
+    def _():
+        gg[0:size, :] = lax.select_n(is_large, gram_s[...], gram_l[...])
+        if size < ROWS:
+            gg[size:, :] = jnp.zeros((ROWS - size, ROWS), F32)
+        each(0, EX_DEV * EX_DEV, lambda i: turn(i, gg, cp))
+
     keep_half = pl.multiple_of(core * half, 8)
     give_half = pl.multiple_of((1 - core) * half, 8)
     keep = pl.multiple_of(core * half + z * quarter, 8)
@@ -347,67 +443,96 @@
     to_z = remote(cp.at[pl.ds(give, quarter)], r2, r_send.at[1], r_recv.at[1], z_peer)
     to_z.start()
 
-    def take(c):
+    to_x = remote(cp.at[pl.ds(keep, quarter)], r3, r_send.at[2], r_recv.at[2], partner)
+    back_z = remote(cf.at[pl.ds(keep, quarter)], cf.at[pl.ds(keep, quarter)], r_send.at[3], r_recv.at[3], z_peer)
+    came_z = remote(cf.at[pl.ds(keep, quarter)], cf.at[pl.ds(give, quarter)], r_send.at[3], r_recv.at[3], z_peer)
+    back_core = remote(
+        cf.at[pl.ds(keep_half, half)], cf.at[pl.ds(keep_half, half)], r_send.at[4], r_recv.at[4], core_peer
+    )
+    came_core = remote(
+        cf.at[pl.ds(keep_half, half)], cf.at[pl.ds(give_half, half)], r_send.at[4], r_recv.at[4], core_peer
+    )
+
+    def panel_part(p, rows, to, sure):
+        first = BASE if sure else 0
+        at = p * rows - BASE * (p if sure else SURE_PANELS)
+        far = fx[pl.ds(pl.multiple_of(at, 16), rows - first), :]
+        to[first:rows, :] += dot_nt(far, xp[X_PANELS - 1 - p])
+
+    scale_g = 1.0 / jnp.sqrt(jnp.full((LEN, LEN), float(D), F32))
+
+    def scaled(i):
+        rows, lanes = spans(i)
+        gg[rows, lanes] = cf[rows, lanes] * scale_g
+
+    def turn_scaled(i):
+        rows, lanes = spans(i)
+        gg[rows, lanes] = jnp.transpose(cf[lanes, rows]) * scale_g
+
+    def take(c, carry):
         send_x(c).wait()
 
-        @pl.when(c + DEPTH < N_X)
+        @pl.when(c + DEPTH < CHUNKS)
         def _():
             send_x(c + DEPTH).start()
 
-        prod[...] += dot_nt(farx[c], xk[c])
-
-    def take_from(first, last):
-        def body(c, carry):
-            take(c)
-            return carry
-
-        lax.fori_loop(first, last, body, 0)
-
-    take_from(0, EVENTS[0])
-    to_z.wait()
-    cp[pl.ds(keep, quarter), :] += r2[...]
-    to_x = remote(cp.at[pl.ds(keep, quarter)], r3, r_send.at[2], r_recv.at[2], partner)
-    to_x.start()
-    take_from(EVENTS[0], EVENTS[1])
-    to_x.wait()
-    cf[pl.ds(keep, quarter), :] = cp[pl.ds(keep, quarter), :] + r3[...]
-    back = remote(cf.at[pl.ds(keep, quarter)], cf.at[pl.ds(keep, quarter)], r_send.at[3], r_recv.at[3], z_peer)
-    back.start()
-    take_from(EVENTS[1], EVENTS[2])
-    back.wait_send()
-    remote(cf.at[pl.ds(keep, quarter)], cf.at[pl.ds(give, quarter)], r_send.at[3], r_recv.at[3], z_peer).wait_recv()
-    back = remote(cf.at[pl.ds(keep_half, half)], cf.at[pl.ds(keep_half, half)], r_send.at[4], r_recv.at[4], core_peer)
-    back.start()
-    back.wait_send()
-    remote(
-        cf.at[pl.ds(keep_half, half)], cf.at[pl.ds(give_half, half)], r_send.at[4], r_recv.at[4], core_peer
-    ).wait_recv()
-    scale_g = 1.0 / jnp.sqrt(jnp.full((LEN, ROWS), float(D), F32))
-
-    @pl.when(hi == 0)
-    def _():
-        for i in range(EX_DEV):
-            gg[i * LEN : (i + 1) * LEN, :] = cf[i * LEN : (i + 1) * LEN, :] * scale_g
-
-    @pl.when(hi == 1)
-    def _():
-        for i in range(EX_DEV):
-            for j in range(EX_DEV):
-                turned = jnp.transpose(cf[j * LEN : (j + 1) * LEN, i * LEN : (i + 1) * LEN])
-                gg[i * LEN : (i + 1) * LEN, j * LEN : (j + 1) * LEN] = turned * scale_g[:, :LEN]
-
-    take_from(EVENTS[2], N_X)
-    scale_x = 1.0 / jnp.sqrt(jnp.full((STEP, LEN), float(FF), F32))
+        @pl.when(c == EVENTS[0])
+        def _():
+            to_z.wait()
+            cp[pl.ds(keep, quarter), :] += r2[...]
+            to_x.start()
+
+        @pl.when(c == EVENTS[1])
+        def _():
+            to_x.wait()
+            cf[pl.ds(keep, quarter), :] = cp[pl.ds(keep, quarter), :] + r3[...]
+            back_z.start()
+
+        @pl.when(c == EVENTS[2])
+        def _():
+            back_z.wait_send()
+            came_z.wait_recv()
+            back_core.start()
+            back_core.wait_send()
+            came_core.wait_recv()
+
+            @pl.when(hi == 0)
+            def _():
+                each(0, EX_DEV * EX_DEV, lambda i: scaled(i))
+
+            @pl.when(hi == 1)
+            def _():
+                each(0, EX_DEV * EX_DEV, lambda i: turn_scaled(i))
+
+        for rows, count, to in ((small, plan.x_panels[1], prod_l), (large, plan.x_panels[0], prod_s)):
+            begin = SURE_PANELS * (rows - BASE)
+
+            def sure_end(k):
+                return jnp.minimum(k * plan.chunk // (rows - BASE), SURE_PANELS)
+
+            def full_end(k):
+                more = jnp.maximum(k * plan.chunk - begin, 0) // rows
+                return SURE_PANELS + jnp.minimum(more, count - SURE_PANELS)
+
+            each(sure_end(c), sure_end(c + 1), functools.partial(panel_part, rows=rows, to=to, sure=True))
+            if count > SURE_PANELS:
+                each(full_end(c), full_end(c + 1), functools.partial(panel_part, rows=rows, to=to, sure=False))
+        return carry
+
+    lax.fori_loop(0, CHUNKS, take, 0)
+    step_rows = 32 if size % 32 == 0 else 16
+    scale_x = 1.0 / jnp.sqrt(jnp.full((step_rows, LEN), float(FF), F32))
 
     def weigh(i):
-        rows = pl.ds(pl.multiple_of(i * STEP, STEP), STEP)
+        rows = pl.ds(pl.multiple_of(i * step_rows, step_rows), step_rows)
         for b in range(EX_DEV):
             lanes = slice(b * LEN, (b + 1) * LEN)
-            product = (prod[rows, lanes] * scale_x) * gg[rows, lanes]
+            gram = lax.select_n(is_large, prod_s[rows, lanes], prod_l[rows, lanes])
+            product = (gram * scale_x) * gg[rows, lanes]
             for a in range(EX_DEV):
                 acc[a : a + 1, lanes] += jnp.sum(product * wl[a, rows, :], axis=0, keepdims=True)
 
-    each(size // STEP, weigh)
+    each(0, size // step_rows, weigh)
     lane = iota((8, LEN), 1)
     wide_row, wide_lane = iota((8, ROWS), 0), iota((8, ROWS), 1)
     right = jnp.zeros((8, ROWS), F32)
@@ -452,7 +577,7 @@
     out_ref[:, 4:8] = whole[:4, 8:12]
     for i in range(1, 16):
         tell(i).wait_send()
-    each(N_G, lambda c: send_g(c).wait_send())
+    each(0, G_CHUNKS, lambda c: send_g(c).wait_send())
 
 
 def vmem():
@@ -473,7 +598,7 @@
         first_kernel,
         name="block_part",
         out_shape=(
-            jax.ShapeDtypeStruct((BASE, N_X * PANEL), BF16),
+            jax.ShapeDtypeStruct((BASE, SURE_PANELS * PANEL), BF16),
             jax.ShapeDtypeStruct((ROWS, ROWS), BF16),
             jax.ShapeDtypeStruct((8, LEN), F32),
             jax.ShapeDtypeStruct((8, LEN), jnp.int32),
@@ -484,7 +609,7 @@
         scratch_shapes=[
             pltpu.VMEM((F_TP, ROWS, WIDE), BF16),
             pltpu.VMEM((D_TP, ROWS, WIDE), BF16),
-            pltpu.VMEM((BASE, N_X * PANEL), BF16),
+            pltpu.VMEM((BASE, SURE_PANELS * PANEL), BF16),
             pltpu.VMEM((LEN, 6 * LEN), F32),
             pltpu.VMEM((LEN, 6 * LEN), F32),
             pltpu.VMEM((LEN // 2, 6 * LEN), F32),
@@ -507,30 +632,39 @@
     )(lengths, feats, grads)
 
 
-def run_second(size, lengths, far_len, blk, pick, near, feats, grads):
+def run_second(number, lengths, far_len, blk, pick, near, feats, grads):
     dma = pltpu.SemaphoreType.DMA
+    plan = Plan(*VARIANTS[number])
+    stream, g_stream = plan.chunk * CHUNKS, plan.g_chunk * G_CHUNKS
+    tall = pltpu.VMEM((plan.large, ROWS), F32)
+    square = pltpu.VMEM((ROWS, ROWS), F32)
     return pl.pallas_call(
-        functools.partial(second_kernel, size),
-        name="cross_part_%d" % size,
+        functools.partial(second_kernel, plan),
+        name="cross_part_%d_%d" % plan.rows,
         out_shape=jax.ShapeDtypeStruct((4, 8), F32),
         in_specs=[smem()] + [hbm()] * 6,
         out_specs=vmem(),
         scratch_shapes=[
-            pltpu.VMEM((2 * N_X, ROWS, PANEL), BF16),
-            pltpu.VMEM((2 * N_G, ROWS, PANEL), BF16),
-            pltpu.VMEM((N_X, size, PANEL), BF16),
-            pltpu.VMEM((N_X, ROWS, PANEL), BF16),
-            pltpu.VMEM((N_G, size, PANEL), BF16),
-            pltpu.VMEM((2, N_G, ROWS, PANEL), BF16),
-            pltpu.VMEM((size, ROWS), F32),
-            pltpu.VMEM((ROWS, ROWS), F32),
-            pltpu.VMEM((ROWS, ROWS), F32),
-            pltpu.VMEM((size // 2, ROWS), F32),
-            pltpu.VMEM((size // 4, ROWS), F32),
-            pltpu.VMEM((size // 4, ROWS), F32),
-            pltpu.VMEM((N_X, size, PANEL), BF16),
-            pltpu.VMEM((size, ROWS), F32),
-            pltpu.VMEM((EX_DEV, size, LEN), F32),
+            pltpu.VMEM((X_PANELS, ROWS, PANEL), BF16),
+            pltpu.VMEM((G_PANELS // 2, ROWS, 2 * NARROW), BF16),
+            pltpu.VMEM((X_PANELS, ROWS, PANEL), BF16),
+            pltpu.VMEM((G_PANELS, ROWS, NARROW), BF16),
+            pltpu.VMEM((stream, PANEL), BF16),
+            pltpu.VMEM((g_stream, NARROW), BF16),
+            pltpu.VMEM((stream, PANEL), BF16),
+            pltpu.VMEM((g_stream, NARROW), BF16),
+            pltpu.VMEM((SURE_PANELS, BASE, PANEL), BF16),
+            square,
+            square,
+            square,
+            pltpu.VMEM((plan.grid // 2, ROWS), F32),
+            pltpu.VMEM((plan.grid // 4, ROWS), F32),
+            pltpu.VMEM((plan.grid // 4, ROWS), F32),
+            tall,
+            tall,
+            tall,
+            tall,
+            pltpu.VMEM((EX_DEV, plan.large, LEN), F32),
             pltpu.VMEM((8, ROWS), F32),
             pltpu.VMEM((8, LEN), F32),
             pltpu.VMEM((16, 8, LEN), F32),
@@ -538,20 +672,20 @@
             pltpu.VMEM((8, LEN), jnp.int32),
             pltpu.VMEM((8, LEN), F32),
             dma((3,)),
-            dma((2 * N_G,)),
-            dma((2 * N_X,)),
-            dma((N_X,)),
-            dma((N_G,)),
-            dma((N_G,)),
-            dma((N_X,)),
-            dma((N_X,)),
+            dma((G_PANELS,)),
+            dma((X_PANELS,)),
+            dma((SURE_PANELS,)),
+            dma((G_CHUNKS,)),
+            dma((G_CHUNKS,)),
+            dma((CHUNKS,)),
+            dma((CHUNKS,)),
             dma((5,)),
             dma((5,)),
             dma((16,)),
             dma((16,)),
         ],
         compiler_params=pltpu.CompilerParams(
-            collective_id=size // STEP, has_side_effects=True, vmem_limit_bytes=56 << 20
+            collective_id=number + 1, has_side_effects=True, vmem_limit_bytes=60 << 20
         ),
     )(lengths, far_len, blk, pick, near, feats, grads)
 
@@ -559,7 +693,7 @@
 def on_device(activations, out_grads, lengths):
     feats, grads = activations[0], out_grads[0]
     near, pick, blk, far_len, which = run_first(lengths, feats, grads)
-    branches = [functools.partial(run_second, size) for size in SIZES]
+    branches = [functools.partial(run_second, number) for number in range(len(VARIANTS))]
     out = lax.switch(which[0], branches, lengths, far_len, blk, pick, near, feats, grads)
     return out[:, 4:8], out[:, 0:4]
 

time: 115 us -> 119 us (1.035)
  Pallas kernels: 112 us -> 117 us
    pallas_call x1, Pallas kernels: 91.6 us -> 96.6 us  [run_second(): pl.pallas_call(functools.partial(second_kernel, plan), name='cross_part_%...]
where the time goes in v3:
time: 119 us
  Pallas kernels  117 us (98%)
  between operations  1.31 us (1%)
    pallas_call x1, Pallas kernels, run_second(): pl.pallas_call(functools.partial(second_kernel, plan), name='cross_part_%...  96.6 us
    pallas_call x1, Pallas kernels, run_first(): pl.pallas_call(first_kernel, name='block_part', out_shape=(jax.ShapeDtype...  20.1 us

profile of v3, /device:TPU:1, one launch (start us, length us, event | category | flops | bytes accessed | tf_op | source)
XLA Modules:
  0.0 119.2 jit_solution(6384547995719041977)
XLA Ops:
  0.6 0.0 copy-start.1
  0.6 0.0 copy-start
  0.6 20.1 %block_part.1 = (bf16[64,2560]{1,0:T(8,128)(2,1)S(1)}, bf16[512,512]{1,0:T(8,128)(2,1)S(1)}, f32[8,128]{1,0:T(8,128)S(1)}, s32[8,128]{1,0:T(8,128)S(1)}, s32[1]{0:T(128)}) custom-call(s32[4]{0:T(128)} %lens.1, bf16[512,7168]{1,0:T(8,128)(2,1)} %bitcast.3, bf16[512,2048]{1,0:T(8,128)(2,1)} %bitcast.12), custom_call_target="tpu_custom_call" | custom-call | tf_op jit(solution)/shard_map/block_part/pallas_call | solution.py:597
  21.4 0.0 copy-done.1
  21.4 0.0 copy-done
  21.4 97.1 %conditional.1 = (f32[4,8]{1,0:T(4,128)S(1)}) conditional(s32[]{:T(128)} %bitcast.2, (s32[4]{0:T(128)S(1)}, s32[8,128]{1,0:T(8,128)S(1)}, f32[8,128]{1,0:T(8,128)S(1)}, bf16[512,512]{1,0:T(8,128)(2,1)S(1)}, bf16[64,2560]{1,0:T(8,128)(2,1)S(1)}, /*index=5*/bf16[512,7168]{1,0:T(8,128)(2,1)}, ...), branch_computations={%region_0.0_spmd, %region_1.0_spmd, %region_2.0_spmd, %region_3.0_... | conditional | bytes 8 | solution.py:697
  21.7 96.6 %cross_part_448_384.1 = f32[4,8]{1,0:T(4,128)S(1)} custom-call(s32[4]{0:T(128)S(1)} %get-tuple-element.156.lens, s32[8,128]{1,0:T(8,128)S(1)} %get-tuple-element.157.far_len_hbm, f32[8,128]{1,0:T(8,128)S(1)} %get-tuple-element.158.blk_hbm, bf16[512,512]{1,0:T(8,128)(2,1)S(1)} %get-tuple-element.159.pick_hbm, ...), custom_call_target="tpu_custom_call" | custom-call | tf_op jit(solution)/shard_map/cond/branch_5_fun/cross_part_448_384/pallas_call | solution.py:641
  118.6 0.7 fusion
Async XLA Ops:
  0.6 20.8 %copy-start.1 = (s32[4]{0:T(128)S(1)}, s32[4]{0:T(128)}, u32[]{:S(2)}) copy-start(s32[4]{0:T(128)} %lens.1) | copy-start | bytes 52
  0.6 20.8 %copy-start = (bf16[1,512,2048]{2,1,0:T(8,128)(2,1)S(1)}, bf16[1,512,2048]{2,1,0:T(8,128)(2,1)}, u32[]{:S(2)}) copy-start(bf16[1,512,2048]{2,1,0:T(8,128)(2,1)} %param.12) | copy-start | bytes 6291460

commit v4 on v3

--- a/solution.py
+++ b/solution.py
@@ -21,12 +21,10 @@
 G_PANELS = 16
 SURE = 16
 BASE = EX_DEV * SURE
-SURE_PANELS = 10
-CHUNKS = 14
+SURE_PANELS = 12
 G_CHUNKS = 2
-DEPTH = 3
+DEPTH = 5
 TURN = 288
-EVENTS = (1, 6, 9)
 VARIANTS = (
     (400, 304),
     (416, 320),
@@ -114,6 +112,15 @@
     for j in range(EX_DEV):
         mine = jnp.where(row == j, counts[j], mine)
     lt[...] = mine
+    xd[...] = jnp.zeros_like(xd)
+    gd[...] = jnp.zeros_like(gd)
+
+    def gram_g(j, carry):
+        load(g_hbm, graw, j, 0).wait()
+        block_tiles(graw, j, gd)
+        return carry
+
+    lax.fori_loop(0, D_TP, gram_g, 0)
     met()
     for i, peer in enumerate(x_peers):
         remote(lt, lx.at[i], l_send.at[i], l_recv.at[i], peer).start()
@@ -126,15 +133,6 @@
 
     for j in range(EX_DEV):
         send_x(j).start()
-    xd[...] = jnp.zeros_like(xd)
-    gd[...] = jnp.zeros_like(gd)
-
-    def gram_g(j, carry):
-        load(g_hbm, graw, j, 0).wait()
-        block_tiles(graw, j, gd)
-        return carry
-
-    lax.fori_loop(0, D_TP, gram_g, 0)
     half = LEN // 2
     keep = pl.multiple_of(core * half, half)
     give = pl.multiple_of((1 - core) * half, half)
@@ -226,7 +224,10 @@
         self.x_panels = (c, X_PANELS - c)
         self.rows = (large, small)
         ends = [self.offset(r, n) for r, n in zip(self.rows, self.x_panels)]
-        self.chunk = up(up(max(ends), 16) // 16, CHUNKS) // CHUNKS * 16
+        units = up(max(ends), 16) // 16
+        self.chunks = min(range(11, 18), key=lambda n: (up(units, n), -n))
+        self.chunk = up(units, self.chunks) // self.chunks * 16
+        self.events = (1, self.chunks * 6 // 14, self.chunks * 9 // 14)
         g_ends = [r * n for r, n in zip(self.rows, self.g_panels)]
         self.g_chunk = up(max(g_ends) // 16, G_CHUNKS) // G_CHUNKS * 16
 
@@ -250,7 +251,7 @@
     plan, lens, far_len_hbm, blk_hbm, pick_hbm, near_hbm, x_hbm, g_hbm,
     out_ref,
     xraw, graw, xp, gp, sx, sg, fx, fg, nr, cp, cf, gg, r1, r2, r3, prod_l, prod_s, gram_l, gram_s,
-    wl, acc, tile, gather, pick, far_len, blk_ref,
+    wl, acc, right_ref, tile, gather, pick, far_len, blk_ref,
     in_sem, ld_sem, lx_sem, near_sem, g_send, g_recv, x_send, x_recv, r_send, r_recv, t_send, t_recv,
 ):
     large, small = plan.rows
@@ -363,7 +364,7 @@
 
         @pl.when(c == plan.x_panels[1] - 1)
         def _():
-            fill(sx, xp, plan.chunk, CHUNKS, x_bounds, x_first)
+            fill(sx, xp, plan.chunk, plan.chunks, x_bounds, x_first)
             each(0, DEPTH, lambda k: send_x(k).start())
 
     each(0, X_PANELS, all_x)
@@ -380,6 +381,18 @@
         cp[size:, :] = jnp.zeros((ROWS - size, ROWS), F32)
         cf[size:, :] = jnp.zeros((ROWS - size, ROWS), F32)
     acc[...] = jnp.zeros_like(acc)
+    wide_row, wide_lane = iota((8, ROWS), 0), iota((8, ROWS), 1)
+    right = jnp.zeros((8, ROWS), F32)
+    begin = jnp.int32(BASE)
+    for b in range(EX_DEV):
+        count = lens[b]
+        inverse = 1.0 / jnp.sqrt(jnp.full((8, ROWS), count.astype(F32), F32))
+        end = begin + count - SURE
+        sure = (wide_lane >= b * SURE) & (wide_lane < (b + 1) * SURE)
+        inside = (wide_row == b) & (sure | ((wide_lane >= begin) & (wide_lane < end)))
+        right = jnp.where(inside, inverse, right)
+        begin = end
+    right_ref[...] = right
     each(0, SURE_PANELS, lambda j: load_near(j).wait())
     def clear(i):
         rows = pl.ds(pl.multiple_of(i * 16, 16), 16)
@@ -472,23 +485,23 @@
     def take(c, carry):
         send_x(c).wait()
 
-        @pl.when(c + DEPTH < CHUNKS)
+        @pl.when(c + DEPTH < plan.chunks)
         def _():
             send_x(c + DEPTH).start()
 
-        @pl.when(c == EVENTS[0])
+        @pl.when(c == plan.events[0])
         def _():
             to_z.wait()
             cp[pl.ds(keep, quarter), :] += r2[...]
             to_x.start()
 
-        @pl.when(c == EVENTS[1])
+        @pl.when(c == plan.events[1])
         def _():
             to_x.wait()
             cf[pl.ds(keep, quarter), :] = cp[pl.ds(keep, quarter), :] + r3[...]
             back_z.start()
 
-        @pl.when(c == EVENTS[2])
+        @pl.when(c == plan.events[2])
         def _():
             back_z.wait_send()
             came_z.wait_recv()
@@ -519,7 +532,7 @@
                 each(full_end(c), full_end(c + 1), functools.partial(panel_part, rows=rows, to=to, sure=False))
         return carry
 
-    lax.fori_loop(0, CHUNKS, take, 0)
+    lax.fori_loop(0, plan.chunks, take, 0)
     step_rows = 32 if size % 32 == 0 else 16
     scale_x = 1.0 / jnp.sqrt(jnp.full((step_rows, LEN), float(FF), F32))
 
@@ -534,18 +547,7 @@
 
     each(0, size // step_rows, weigh)
     lane = iota((8, LEN), 1)
-    wide_row, wide_lane = iota((8, ROWS), 0), iota((8, ROWS), 1)
-    right = jnp.zeros((8, ROWS), F32)
-    begin = jnp.int32(BASE)
-    for b in range(EX_DEV):
-        count = lens[b]
-        inverse = 1.0 / jnp.sqrt(jnp.full((8, ROWS), count.astype(F32), F32))
-        end = begin + count - SURE
-        sure = (wide_lane >= b * SURE) & (wide_lane < (b + 1) * SURE)
-        inside = (wide_row == b) & (sure | ((wide_lane >= begin) & (wide_lane < end)))
-        right = jnp.where(inside, inverse, right)
-        begin = end
-    found = acc[...]
+    found, right = acc[...], right_ref[...]
     out = blk_ref[...]
     for a in range(EX_DEV):
         summed = jnp.sum(right * found[a : a + 1, :], axis=1, keepdims=True)
@@ -635,7 +637,7 @@
 def run_second(number, lengths, far_len, blk, pick, near, feats, grads):
     dma = pltpu.SemaphoreType.DMA
     plan = Plan(*VARIANTS[number])
-    stream, g_stream = plan.chunk * CHUNKS, plan.g_chunk * G_CHUNKS
+    stream, g_stream = plan.chunk * plan.chunks, plan.g_chunk * G_CHUNKS
     tall = pltpu.VMEM((plan.large, ROWS), F32)
     square = pltpu.VMEM((ROWS, ROWS), F32)
     return pl.pallas_call(
@@ -666,6 +668,7 @@
             tall,
             pltpu.VMEM((EX_DEV, plan.large, LEN), F32),
             pltpu.VMEM((8, ROWS), F32),
+            pltpu.VMEM((8, ROWS), F32),
             pltpu.VMEM((8, LEN), F32),
             pltpu.VMEM((16, 8, LEN), F32),
             pltpu.VMEM((ROWS, ROWS), BF16),
@@ -677,8 +680,8 @@
             dma((SURE_PANELS,)),
             dma((G_CHUNKS,)),
             dma((G_CHUNKS,)),
-            dma((CHUNKS,)),
-            dma((CHUNKS,)),
+            dma((plan.chunks,)),
+            dma((plan.chunks,)),
             dma((5,)),
             dma((5,)),
             dma((16,)),

time: 119 us -> 110 us (0.924)
  Pallas kernels: 117 us -> 107 us
    pallas_call x1, Pallas kernels: 96.6 us -> 86.4 us  [run_second(): pl.pallas_call(functools.partial(second_kernel, plan), name='cross_part_%...]
where the time goes in v4:
time: 110 us; the launch traced here: 109 us
  Pallas kernels  107 us (97%)
  between operations  1.31 us (1%)
    pallas_call x1, Pallas kernels, run_second(): pl.pallas_call(functools.partial(second_kernel, plan), name='cross_part_%...  86.4 us
    pallas_call x1, Pallas kernels, run_first(): pl.pallas_call(first_kernel, name='block_part', out_shape=(jax.ShapeDtype...  20.2 us

profile of v4, /device:TPU:1, one launch (start us, length us, event | category | flops | bytes accessed | tf_op | source)
XLA Modules:
  0.0 109.4 jit_solution(3539663226352909247)
XLA Ops:
  0.6 0.0 copy-start.1
  0.6 0.0 copy-start
  0.6 20.2 %block_part.1 = (bf16[64,3072]{1,0:T(8,128)(2,1)S(1)}, bf16[512,512]{1,0:T(8,128)(2,1)S(1)}, f32[8,128]{1,0:T(8,128)S(1)}, s32[8,128]{1,0:T(8,128)S(1)}, s32[1]{0:T(128)}) custom-call(s32[4]{0:T(128)} %lens.1, bf16[512,7168]{1,0:T(8,128)(2,1)} %bitcast.3, bf16[512,2048]{1,0:T(8,128)(2,1)} %bitcast.12), custom_call_target="tpu_custom_call" | custom-call | tf_op jit(solution)/shard_map/block_part/pallas_call | solution.py:599
  21.5 0.0 copy-done.1
  21.5 0.0 copy-done
  21.5 87.2 %conditional.1 = (f32[4,8]{1,0:T(4,128)S(1)}) conditional(s32[]{:T(128)} %bitcast.2, (s32[4]{0:T(128)S(1)}, s32[8,128]{1,0:T(8,128)S(1)}, f32[8,128]{1,0:T(8,128)S(1)}, bf16[512,512]{1,0:T(8,128)(2,1)S(1)}, bf16[64,3072]{1,0:T(8,128)(2,1)S(1)}, /*index=5*/bf16[512,7168]{1,0:T(8,128)(2,1)}, ...), branch_computations={%region_0.0_spmd, %region_1.0_spmd, %region_2.0_spmd, %region_3.0_... | conditional | bytes 8 | solution.py:700
  21.8 86.4 %cross_part_448_336.1 = f32[4,8]{1,0:T(4,128)S(1)} custom-call(s32[4]{0:T(128)S(1)} %get-tuple-element.142.lens, s32[8,128]{1,0:T(8,128)S(1)} %get-tuple-element.143.far_len_hbm, f32[8,128]{1,0:T(8,128)S(1)} %get-tuple-element.144.blk_hbm, bf16[512,512]{1,0:T(8,128)(2,1)S(1)} %get-tuple-element.145.pick_hbm, ...), custom_call_target="tpu_custom_call" | custom-call | tf_op jit(solution)/shard_map/cond/branch_3_fun/cross_part_448_336/pallas_call | solution.py:643
  108.7 0.7 fusion
Async XLA Ops:
  0.6 20.9 %copy-start.1 = (s32[4]{0:T(128)S(1)}, s32[4]{0:T(128)}, u32[]{:S(2)}) copy-start(s32[4]{0:T(128)} %lens.1) | copy-start | bytes 52
  0.6 20.9 %copy-start = (bf16[1,512,2048]{2,1,0:T(8,128)(2,1)S(1)}, bf16[1,512,2048]{2,1,0:T(8,128)(2,1)}, u32[]{:S(2)}) copy-start(bf16[1,512,2048]{2,1,0:T(8,128)(2,1)} %param.12) | copy-start | bytes 6291460

commit v5 on v4

--- a/solution.py
+++ b/solution.py
@@ -26,6 +26,7 @@
 DEPTH = 5
 TURN = 288
 VARIANTS = (
+    (384, 288),
     (400, 304),
     (416, 320),
     (400, 352),
@@ -168,10 +169,10 @@
         return carry
 
     lax.fori_loop(0, F_TP, gram_x, 0)
+    swap = remote(xd.at[pl.ds(give, half)], r_back, d_send.at[2], d_recv.at[2], core_peer)
+    swap.start()
     to_z.wait()
     gd[pl.ds(keep, half), :] += r_z[...]
-    back = remote(gd.at[pl.ds(keep, half)], r_back, d_send.at[2], d_recv.at[2], core_peer)
-    back.start()
     for i in range(3):
         remote(mt, ly.at[i], l_send.at[3 + i], l_recv.at[3 + i], y_peers[i]).wait_recv()
     most = jnp.maximum(jnp.maximum(mt[...], ly[0]), jnp.maximum(ly[1], ly[2]))
@@ -180,19 +181,20 @@
         fits = (most[4:5, :] <= VARIANTS[i][0]) & (most[5:6, :] <= VARIANTS[i][1])
         which = jnp.where(fits, i, which)
     which_ref[0] = jnp.max(which)
-    back.wait()
-    gd[pl.ds(give, half), :] = r_back[...]
+    swap.wait()
+    xd[pl.ds(keep, half), :] += r_back[...]
     blk = jnp.zeros((8, LEN), F32)
     lane = iota((8, LEN), 1)
-    inner_row = iota((LEN, LEN), 0)
-    inner_lane = iota((LEN, LEN), 1)
-    scale_x = 1.0 / jnp.sqrt(jnp.full((LEN, LEN), float(FF), F32))
-    scale_g = 1.0 / jnp.sqrt(jnp.full((LEN, LEN), float(D), F32))
+    inner_row = iota((half, LEN), 0) + keep
+    inner_lane = iota((half, LEN), 1)
+    scale_x = 1.0 / jnp.sqrt(jnp.full((half, LEN), float(FF), F32))
+    scale_g = 1.0 / jnp.sqrt(jnp.full((half, LEN), float(D), F32))
     inverse = [1.0 / jnp.sqrt(jnp.full((8, LEN), counts[j].astype(F32), F32)) for j in range(EX_DEV)]
     at = 0
     for a in range(EX_DEV - 1):
         for b in range(a + 1, EX_DEV):
-            product = (xd[:, at : at + LEN] * scale_x) * (gd[:, at : at + LEN] * scale_g)
+            rows, lanes = pl.ds(keep, half), slice(at, at + LEN)
+            product = (xd[rows, lanes] * scale_x) * (gd[rows, lanes] * scale_g)
             live = (inner_row < counts[a]) & (inner_lane < counts[b])
             product = jnp.where(live, product, 0.0)
             total = jnp.sum(jnp.sum(product, axis=0, keepdims=True), axis=1, keepdims=True)
@@ -218,6 +220,7 @@
     def __init__(self, large, small):
         self.large, self.small = large, small
         self.grid = up(large, 32)
+        self.lanes = up(small, 128)
         c = min(range(SURE_PANELS, X_PANELS // 2 + 1), key=lambda c: max(c * large, (X_PANELS - c) * small))
         d = min(range(1, G_PANELS // 2 + 1), key=lambda d: max(d * large, (G_PANELS - d) * small))
         self.g_panels = (d, G_PANELS - d)
@@ -378,8 +381,10 @@
 
         each(0, G_PANELS, clear_g)
         each(0, X_PANELS, clear_x)
-        cp[size:, :] = jnp.zeros((ROWS - size, ROWS), F32)
-        cf[size:, :] = jnp.zeros((ROWS - size, ROWS), F32)
+        if plan.grid < ROWS:
+            cf[plan.grid :, :] = jnp.zeros((ROWS - plan.grid, ROWS), F32)
+    if plan.lanes < ROWS:
+        cf[:, plan.lanes :] = jnp.zeros((ROWS, ROWS - plan.lanes), F32)
     acc[...] = jnp.zeros_like(acc)
     wide_row, wide_lane = iota((8, ROWS), 0), iota((8, ROWS), 1)
     right = jnp.zeros((8, ROWS), F32)
@@ -396,10 +401,16 @@
     each(0, SURE_PANELS, lambda j: load_near(j).wait())
     def clear(i):
         rows = pl.ds(pl.multiple_of(i * 16, 16), 16)
-        for ref in (prod_s, prod_l, gram_s, gram_l):
+        for ref in (prod_s, prod_l):
             ref[rows, :] = jnp.zeros((16, ROWS), F32)
 
+    def clear_square(i):
+        rows = pl.ds(pl.multiple_of(i * 16, 16), 16)
+        for ref in (gram_s, gram_l):
+            ref[rows, :] = jnp.zeros((16, ROWS), F32)
+
     each(0, size // 16, clear)
+    each(0, ROWS // 16, clear_square)
 
     def near_part(p):
         prod_s[0:BASE, :] += dot_nt(nr[p], xp[X_PANELS - 1 - p])
@@ -429,41 +440,32 @@
         i, j = i // EX_DEV, lax.rem(i, EX_DEV)
         return pl.ds(pl.multiple_of(i * LEN, LEN), LEN), pl.ds(pl.multiple_of(j * LEN, LEN), LEN)
 
-    def turn(i, source, to):
+    def by_role(i):
         rows, lanes = spans(i)
-        to[rows, lanes] = jnp.transpose(source[lanes, rows])
-
-    @pl.when(hi == 0)
-    def _():
-        cp[0:size, :] = lax.select_n(is_large, gram_s[...], gram_l[...])
-
-    @pl.when(hi == 1)
-    def _():
-        gg[0:size, :] = lax.select_n(is_large, gram_s[...], gram_l[...])
-        if size < ROWS:
-            gg[size:, :] = jnp.zeros((ROWS - size, ROWS), F32)
-        each(0, EX_DEV * EX_DEV, lambda i: turn(i, gg, cp))
-
+        cp[rows, lanes] = lax.select_n(is_large, gram_s[rows, lanes], jnp.transpose(gram_l[lanes, rows]))
+
+    each(0, EX_DEV * EX_DEV, by_role)
+    live = pl.ds(0, plan.lanes)
     keep_half = pl.multiple_of(core * half, 8)
     give_half = pl.multiple_of((1 - core) * half, 8)
     keep = pl.multiple_of(core * half + z * quarter, 8)
     give = pl.multiple_of(core * half + (1 - z) * quarter, 8)
 
-    step = remote(cp.at[pl.ds(give_half, half)], r1, r_send.at[0], r_recv.at[0], core_peer)
+    step = remote(cp.at[pl.ds(give_half, half), live], r1, r_send.at[0], r_recv.at[0], core_peer)
     step.start()
     step.wait()
-    cp[pl.ds(keep_half, half), :] += r1[...]
-    to_z = remote(cp.at[pl.ds(give, quarter)], r2, r_send.at[1], r_recv.at[1], z_peer)
+    cp[pl.ds(keep_half, half), live] += r1[...]
+    to_z = remote(cp.at[pl.ds(give, quarter), live], r2, r_send.at[1], r_recv.at[1], z_peer)
     to_z.start()
 
-    to_x = remote(cp.at[pl.ds(keep, quarter)], r3, r_send.at[2], r_recv.at[2], partner)
-    back_z = remote(cf.at[pl.ds(keep, quarter)], cf.at[pl.ds(keep, quarter)], r_send.at[3], r_recv.at[3], z_peer)
-    came_z = remote(cf.at[pl.ds(keep, quarter)], cf.at[pl.ds(give, quarter)], r_send.at[3], r_recv.at[3], z_peer)
+    to_x = remote(cp.at[pl.ds(keep, quarter), live], r3, r_send.at[2], r_recv.at[2], partner)
+    back_z = remote(cf.at[pl.ds(keep, quarter), live], cf.at[pl.ds(keep, quarter), live], r_send.at[3], r_recv.at[3], z_peer)
+    came_z = remote(cf.at[pl.ds(keep, quarter), live], cf.at[pl.ds(give, quarter), live], r_send.at[3], r_recv.at[3], z_peer)
     back_core = remote(
-        cf.at[pl.ds(keep_half, half)], cf.at[pl.ds(keep_half, half)], r_send.at[4], r_recv.at[4], core_peer
+        cf.at[pl.ds(keep_half, half), live], cf.at[pl.ds(keep_half, half), live], r_send.at[4], r_recv.at[4], core_peer
     )
     came_core = remote(
-        cf.at[pl.ds(keep_half, half)], cf.at[pl.ds(give_half, half)], r_send.at[4], r_recv.at[4], core_peer
+        cf.at[pl.ds(keep_half, half), live], cf.at[pl.ds(give_half, half), live], r_send.at[4], r_recv.at[4], core_peer
     )
 
     def panel_part(p, rows, to, sure):
@@ -476,11 +478,8 @@
 
     def scaled(i):
         rows, lanes = spans(i)
-        gg[rows, lanes] = cf[rows, lanes] * scale_g
-
-    def turn_scaled(i):
-        rows, lanes = spans(i)
-        gg[rows, lanes] = jnp.transpose(cf[lanes, rows]) * scale_g
+        gram = lax.select_n(is_large, cf[rows, lanes], jnp.transpose(cf[lanes, rows]))
+        gg[rows, lanes] = gram * scale_g
 
     def take(c, carry):
         send_x(c).wait()
@@ -492,13 +491,13 @@
         @pl.when(c == plan.events[0])
         def _():
             to_z.wait()
-            cp[pl.ds(keep, quarter), :] += r2[...]
+            cp[pl.ds(keep, quarter), live] += r2[...]
             to_x.start()
 
         @pl.when(c == plan.events[1])
         def _():
             to_x.wait()
-            cf[pl.ds(keep, quarter), :] = cp[pl.ds(keep, quarter), :] + r3[...]
+            cf[pl.ds(keep, quarter), live] = cp[pl.ds(keep, quarter), live] + r3[...]
             back_z.start()
 
         @pl.when(c == plan.events[2])
@@ -509,13 +508,7 @@
             back_core.wait_send()
             came_core.wait_recv()
 
-            @pl.when(hi == 0)
-            def _():
-                each(0, EX_DEV * EX_DEV, lambda i: scaled(i))
-
-            @pl.when(hi == 1)
-            def _():
-                each(0, EX_DEV * EX_DEV, lambda i: turn_scaled(i))
+            each(0, EX_DEV * EX_DEV, scaled)
 
         for rows, count, to in ((small, plan.x_panels[1], prod_l), (large, plan.x_panels[0], prod_s)):
             begin = SURE_PANELS * (rows - BASE)
@@ -659,13 +652,13 @@
             square,
             square,
             square,
-            pltpu.VMEM((plan.grid // 2, ROWS), F32),
-            pltpu.VMEM((plan.grid // 4, ROWS), F32),
-            pltpu.VMEM((plan.grid // 4, ROWS), F32),
+            pltpu.VMEM((plan.grid // 2, plan.lanes), F32),
+            pltpu.VMEM((plan.grid // 4, plan.lanes), F32),
+            pltpu.VMEM((plan.grid // 4, plan.lanes), F32),
             tall,
             tall,
-            tall,
-            tall,
+            square,
+            square,
             pltpu.VMEM((EX_DEV, plan.large, LEN), F32),
             pltpu.VMEM((8, ROWS), F32),
             pltpu.VMEM((8, ROWS), F32),

time: 110 us -> 110 us (level); the launches traced: 109 us -> 112 us
  Pallas kernels: 107 us -> 109 us
    pallas_call x1, Pallas kernels: 86.4 us -> 90.8 us  [run_second(): pl.pallas_call(functools.partial(second_kernel, plan), name='cross_part_%...]
    pallas_call x1, Pallas kernels: 20.2 us -> 18.6 us  [run_first(): pl.pallas_call(first_kernel, name='block_part', out_shape=(jax.ShapeDtype...]
where the time goes in v5:
time: 110 us; the launch traced here: 112 us
  Pallas kernels  109 us (99%)
  between operations  1.24 us (1%)
    pallas_call x1, Pallas kernels, run_second(): pl.pallas_call(functools.partial(second_kernel, plan), name='cross_part_%...  90.8 us
    pallas_call x1, Pallas kernels, run_first(): pl.pallas_call(first_kernel, name='block_part', out_shape=(jax.ShapeDtype...  18.6 us

profile of v5, /device:TPU:1, one launch (start us, length us, event | category | flops | bytes accessed | tf_op | source)
XLA Modules:
  0.0 111.9 jit_solution(14151877842584629292)
XLA Ops:
  0.6 0.0 copy-start.1
  0.6 0.0 copy-start
  0.6 18.6 %block_part.1 = (bf16[64,3072]{1,0:T(8,128)(2,1)S(1)}, bf16[512,512]{1,0:T(8,128)(2,1)S(1)}, f32[8,128]{1,0:T(8,128)S(1)}, s32[8,128]{1,0:T(8,128)S(1)}, s32[1]{0:T(128)}) custom-call(s32[4]{0:T(128)} %lens.1, bf16[512,7168]{1,0:T(8,128)(2,1)} %bitcast.3, bf16[512,2048]{1,0:T(8,128)(2,1)} %bitcast.13), custom_call_target="tpu_custom_call" | custom-call | tf_op jit(solution)/shard_map/block_part/pallas_call | solution.py:592
  19.8 0.0 copy-done.1
  19.8 0.0 copy-done
  19.9 91.4 %conditional.1 = (f32[4,8]{1,0:T(4,128)S(1)}) conditional(s32[]{:T(128)} %bitcast.2, (s32[4]{0:T(128)S(1)}, s32[8,128]{1,0:T(8,128)S(1)}, f32[8,128]{1,0:T(8,128)S(1)}, bf16[512,512]{1,0:T(8,128)(2,1)S(1)}, bf16[64,3072]{1,0:T(8,128)(2,1)S(1)}, /*index=5*/bf16[512,7168]{1,0:T(8,128)(2,1)}, ...), branch_computations={%region_0.0_spmd, %region_1.0_spmd, %region_2.0_spmd, %region_3.0_... | conditional | bytes 8 | solution.py:693
  20.1 90.8 %cross_part_464_352.1 = f32[4,8]{1,0:T(4,128)S(1)} custom-call(s32[4]{0:T(128)S(1)} %get-tuple-element.171.lens, s32[8,128]{1,0:T(8,128)S(1)} %get-tuple-element.172.far_len_hbm, f32[8,128]{1,0:T(8,128)S(1)} %get-tuple-element.173.blk_hbm, bf16[512,512]{1,0:T(8,128)(2,1)S(1)} %get-tuple-element.174.pick_hbm, ...), custom_call_target="tpu_custom_call" | custom-call | tf_op jit(solution)/shard_map/cond/branch_5_fun/cross_part_464_352/pallas_call | solution.py:636
  111.2 0.7 fusion
Async XLA Ops:
  0.6 19.2 %copy-start.1 = (s32[4]{0:T(128)S(1)}, s32[4]{0:T(128)}, u32[]{:S(2)}) copy-start(s32[4]{0:T(128)} %lens.1) | copy-start | bytes 52
  0.6 19.2 %copy-start = (bf16[1,512,2048]{2,1,0:T(8,128)(2,1)S(1)}, bf16[1,512,2048]{2,1,0:T(8,128)(2,1)}, u32[]{:S(2)}) copy-start(bf16[1,512,2048]{2,1,0:T(8,128)(2,1)} %param.13) | copy-start | bytes 6291460
